TPU v7x, 256 devices: a whole 4x4x8 slice. The times are simulated.
256 devices in a mesh: span: 32 (over z, x), elem: 8 (over y, core).
Axes of the slice: x: 4, y: 4, z: 8, core: 2. Of those that a mesh axis runs over, the one named last changes fastest.
Arguments:
- species: float32 [81, 3, 512, 1024], P(None, None, 'span', 'elem'), may hold values from 0.02 to 0.3
- laplacian: float32 [81, 3, 512, 1024], P(None, None, 'span', 'elem'), may hold values from -6 to 6
- binary: float32 [3, 4], replicated, may hold values from 0.3 to 3
- dref: float32 [3], replicated, may hold values from 0.5 to 2
- stiff_eig: float32 [9], replicated, may hold values from 0.02 to 3
- basis: float32 [9, 9], replicated, may hold values from -1 to 1, as said below
- rounds: int32 [256], replicated, may hold values from 1 to 4
- adjacency: int32 [1024, 4], P('elem'), may hold values from 0 to 1023, as said below
- edge_map: int32 [1024, 4], P('elem'), may hold values from 0 to 3
Outputs:
- updated: float32 [81, 3, 512, 1024], P(None, None, 'span', 'elem')
Inputs may be any that keep to these rules, and one draw needn't show every extreme that they name: basis is an orthogonal matrix. The elements form a periodic mesh of 16 columns and 8 * 8 rows; each index of elem holds 8 whole rows in some order. adjacency is symmetric: element e lies across edge edge_map[e, j] of element adjacency[e, j]. The element across an edge lies on the same index of elem or on the one just before or after it, cyclically; exactly 16 elements of each index have an edge facing the next index and 16 one facing the previous, one such edge each.
All inputs are finite; a program needn't handle non-finite values.
Results may differ from a plain program's by a relative error of at most 0.0001.
Values sent between devices are 32-bit elements; how exact they have to be, the bound alone decides.
A program may use at most 128 MiB of HBM per device.

v0:
```python
import jax
import jax.numpy as jnp
import numpy as np
from jax import lax
from jax.sharding import PartitionSpec as P

coupling = 0.2
highest = lax.Precision.HIGHEST
two_pi = 6.283185307179586


def extended(block, sides, width):
    for axis, dim in sides:
        count = lax.axis_size(axis)
        forward = [(i, i + 1) for i in range(count - 1)]
        forward.append((count - 1, 0))
        backward = [(target, source) for source, target in forward]
        low = lax.ppermute(
            lax.slice_in_dim(block, block.shape[dim] - width, None, axis=dim), axis, forward
        )
        high = lax.ppermute(lax.slice_in_dim(block, 0, width, axis=dim), axis, backward)
        block = jnp.concatenate([low, block, high], axis=dim)
    return block


def edge_lists(per_side):
    last_node = per_side - 1
    bottom = [i for i in range(per_side)]
    right_edge = [i * per_side + last_node for i in range(per_side)]
    top_edge = [last_node * per_side + last_node - i for i in range(per_side)]
    left_edge = [(last_node - i) * per_side for i in range(per_side)]
    return [bottom, right_edge, top_edge, left_edge]


def edge_matrix(per_side):
    edge_table = np.zeros((4, per_side, per_side * per_side), np.float32)
    for edge_id, node_list in enumerate(edge_lists(per_side)):
        for i, node_id in enumerate(node_list):
            edge_table[edge_id, i, node_id] = 1.0
    return edge_table


def mixture_source(species, laplacian, binary, dref):
    n_species = species.shape[1]
    bath_share = 1.0 - jnp.sum(species, axis=1)
    source_parts = []
    for s in range(n_species):
        resistance = bath_share / binary[s, n_species]
        for j in range(n_species):
            if j != s:
                resistance = resistance + species[:, j] / binary[s, j]
        mixture = (1.0 - species[:, s]) / resistance
        source_parts.append((species[:, s] + (mixture - dref[s]) * laplacian[:, s]) / dref[s])
    return jnp.stack(source_parts, axis=1)


def block_inverse(values, kron_basis, inverse_diag):
    n_nodes = values.shape[0]
    inner_part = (
        jnp.dot(kron_basis.T, values.reshape(n_nodes, -1), precision=highest).reshape(values.shape)
        * inverse_diag
    )
    return jnp.dot(kron_basis, inner_part.reshape(n_nodes, -1), precision=highest).reshape(
        values.shape
    )


def transform_tables(col_mode, col_part, planes):
    plane_ids = jnp.arange(planes, dtype=jnp.int32)
    phase_id = plane_ids[:, None] * col_mode[None, :] % planes
    angles = phase_id.astype(jnp.float32) * (two_pi / planes)
    trig_table = jnp.where(col_part[None, :] == 0, jnp.cos(angles), -jnp.sin(angles))
    weights = jnp.where(col_mode == 0, 1.0, 2.0).astype(jnp.float32)
    return (trig_table / planes, (trig_table * weights[None, :]).T)


def body(species, laplacian, binary, dref, stiff_eig, basis, rounds, adjacency, edge_map):
    per_side = basis.shape[0]
    n_nodes = per_side * per_side
    n_span = lax.axis_size("span")
    n_elem = lax.axis_size("elem")
    planes = species.shape[2] * n_span
    n_modes = planes // 2
    per_device = n_modes // n_span
    half_tile = per_device // 2
    own_count = adjacency.shape[0]
    source = mixture_source(species, laplacian, binary, dref)
    assign = jnp.arange(n_modes, dtype=jnp.int32).reshape(n_span, per_device)
    tile_count = 1
    col_mode = jnp.broadcast_to(
        assign.reshape(n_span, 2, 1, half_tile), (n_span, 2, 2, half_tile)
    ).reshape(planes)
    col_part = jnp.broadcast_to(
        jnp.arange(2, dtype=jnp.int32).reshape(1, 1, 2, 1), (n_span, 2, 2, half_tile)
    ).reshape(planes)
    forward, backward = transform_tables(col_mode, col_part, planes)
    source_swapped = jnp.transpose(source, (0, 1, 3, 2))
    coeffs = jnp.einsum(
        "nsez,zr->nser",
        lax.all_to_all(source_swapped, "span", split_axis=2, concat_axis=3, tiled=True),
        forward,
        precision=highest,
    )
    exchanged = lax.all_to_all(coeffs, "span", split_axis=3, concat_axis=2, tiled=True)
    modal_rhs = jnp.transpose(exchanged, (0, 1, 3, 2))
    columns = 2 * per_device
    my_modes = lax.dynamic_slice_in_dim(col_mode, lax.axis_index("span") * columns, columns)
    my_rounds = rounds[my_modes]
    wavenumber = my_modes.astype(jnp.float32) * (8.0 / planes)
    shifts = 1.0 / dref[:, None] + (wavenumber * wavenumber)[None, :]
    eig_sum = (stiff_eig[:, None] + stiff_eig[None, :]).reshape(n_nodes)
    inverse_diag = 1.0 / (shifts[None, :, :, None] + eig_sum[:, None, None, None])
    kron_basis = (basis[:, None, :, None] * basis[None, :, None, :]).reshape(n_nodes, n_nodes)
    flat_index = np.array(edge_lists(per_side)).reshape(-1)
    scatter_table = jnp.asarray(edge_matrix(per_side))
    owners = adjacency // own_count
    offset = (owners - lax.axis_index("elem") + n_elem) % n_elem
    local_id = adjacency % own_count
    position = jnp.where(
        offset == 0,
        own_count + local_id,
        jnp.where(offset == 1, 2 * own_count + local_id, local_id),
    )

    def gather_pool(traces):
        return extended(traces, (("elem", 4),), own_count)

    def couple(modal_field):
        traces = modal_field[flat_index].reshape((4, per_side) + modal_field.shape[1:])
        across = gather_pool(traces)[edge_map, :, :, :, position][:, :, ::-1]
        return jnp.einsum("jtn,ejtsc->nsce", scatter_table, across, precision=highest)

    tile_modes = assign.reshape(n_span, tile_count, per_device // tile_count)
    sweep_bound = jnp.max(rounds[tile_modes[:, 0].reshape(-1)])
    initial = block_inverse(modal_rhs, kron_basis, inverse_diag)

    def sweep_once(sweep_id, modal_field):
        proposal = block_inverse(
            modal_rhs + coupling * couple(modal_field), kron_basis, inverse_diag
        )
        return jnp.where(sweep_id < my_rounds[:, None], proposal, modal_field)

    solved = lax.fori_loop(1, sweep_bound, sweep_once, initial)
    solution_swapped = jnp.transpose(solved, (0, 1, 3, 2))
    values = jnp.einsum(
        "nser,rz->nsez",
        lax.all_to_all(solution_swapped, "span", split_axis=2, concat_axis=3, tiled=True),
        backward,
        precision=highest,
    )
    returned = lax.all_to_all(values, "span", split_axis=3, concat_axis=2, tiled=True)
    return jnp.transpose(returned, (0, 1, 3, 2))


def solution(mesh):
    return jax.shard_map(
        body,
        mesh=mesh,
        in_specs=(
            P(None, None, "span", "elem"),
            P(None, None, "span", "elem"),
            P(),
            P(),
            P(),
            P(),
            P(),
            P("elem", None),
            P("elem", None),
        ),
        out_specs=P(None, None, "span", "elem"),
        check_vma=False,
    )
```

profile of v0, /device:TPU:6, one launch (start us, length us, event | category | flops | bytes accessed | tf_op | source)
XLA Modules:
  0.0 673.9 jit_solution(4324216271169737449)
XLA Ops:
  17.1 12.0 %all-to-all-start = ((f32[81,3,128,16]{0,3,1,2:T(8,128)}), f32[81,3,128,16]{0,3,1,2:T(8,128)S(1)}, u32[]{:S(2)}, u32[]{:S(2)}) async-start(f32[81,3,128,16]{0,3,1,2:T(8,128)} %copy.73), calls=%async_computation | async-start | bytes 6291456 | tf_op jit(solution)/shard_map/all_to_all | solution.py:100
  29.5 70.7 %all-to-all-done = f32[81,3,128,16]{0,3,1,2:T(8,128)S(1)} async-done(((f32[81,3,128,16]{0,3,1,2:T(8,128)}), f32[81,3,128,16]{0,3,1,2:T(8,128)S(1)}, u32[]{:S(2)}, u32[]{:S(2)}) %all-to-all-start) | async-done | bytes 1990688 | tf_op jit(solution)/shard_map/all_to_all | solution.py:100
  100.6 9.5 %fusion.22 = f32[81,3,4,512]{3,0,2,1:T(8,128)S(1)} fusion(f32[81,3,4,512]{0,3,2,1:T(8,128)S(1)} %bitcast.285, s32[512]{0:T(512)S(1)} %mul.125, pred[512]{0:T(512)(128)(4,1)S(1)} %eq.42), kind=kOutput, calls=%fused_computation.37 | convolution fusion | flops 3062104064 | bytes 3983872 | tf_op jit(solution)/shard_map/nsez,zr->nser/dot_general | solution.py:98
  113.0 21.9 %all-to-all-start.1 = ((f32[81,3,4,512]{0,2,1,3:T(4,128)}), f32[81,3,4,512]{0,2,1,3:T(4,128)S(1)}, u32[]{:S(2)}, u32[]{:S(2)}) async-start(f32[81,3,4,512]{0,2,1,3:T(4,128)} %copy.77), calls=%async_computation.1 | async-start | bytes 6291456 | tf_op jit(solution)/shard_map/all_to_all | solution.py:104
  144.5 61.5 %all-to-all-done.1 = f32[81,3,4,512]{0,2,1,3:T(4,128)S(1)} async-done(((f32[81,3,4,512]{0,2,1,3:T(4,128)}), f32[81,3,4,512]{0,2,1,3:T(4,128)S(1)}, u32[]{:S(2)}, u32[]{:S(2)}) %all-to-all-start.1) | async-done | bytes 1990688 | tf_op jit(solution)/shard_map/all_to_all | solution.py:104
  218.8 280.1 %while.12 = (s32[]{:T(128)}, f32[81,3,16,128]{3,2,1,0:T(8,128)S(1)}, s32[]{:T(128)}, s32[16]{0:T(128)S(1)}, s32[128,4]{1,0:T(8,128)S(1)}, /*index=5*/s32[128,4]{...) while((s32[]{:T(128)}, ...), condition=%wide.region_3.4_spmd.clone.clone, body=%wide.region_2.3_spmd.sunk.clone.clone.sunk | while | flops 1185788416 | bytes 103511216 | solution.py:143
  238.7 18.7 %copy.144 = f32[4,9,3,16,384]{3,2,4,1,0:T(4,128)} copy(f32[4,9,3,16,384]{4,3,2,1,0:T(8,128)S(1)} %pad_maximum_fusion.2) | data formatting | bytes 5308416 | tf_op jit(solution)/shard_map/while/body/concatenate | solution.py:22
  257.4 22.1 %gather_fusion.1 = f32[512,9,3,16]{3,2,1,0:T(4,128)} fusion(f32[4,9,3,16,384]{3,2,4,1,0:T(4,128)} %copy.144, s32[512]{0:T(512)S(1)} %reshape.295), kind=kCustom, calls=%fused_computation.1.clone.clone.1 | custom fusion | bytes 1773568 | tf_op jit(solution)/shard_map/while/body/gather | solution.py:130
  279.5 7.4 %copy.145 = f32[512,9,3,16]{3,0,2,1:T(8,128)} copy(f32[512,9,3,16]{3,2,1,0:T(4,128)} %gather_fusion.1) | data formatting | bytes 1769472 | tf_op jit(solution)/shard_map/while/body/gather | solution.py:130
  286.9 6.7 rev.7
  293.6 7.3 %copy.146 = f32[128,4,9,3,16]{0,2,1,4,3:T(8,128)S(1)} copy(f32[128,4,9,3,16]{4,1,0,3,2:T(4,128)} %rev.7) | data formatting | bytes 1769472 | tf_op jit(solution)/shard_map/while/body/rev | solution.py:130
  330.9 18.7 %copy.144 = f32[4,9,3,16,384]{3,2,4,1,0:T(4,128)} copy(f32[4,9,3,16,384]{4,3,2,1,0:T(8,128)S(1)} %pad_maximum_fusion.2) | data formatting | bytes 5308416 | tf_op jit(solution)/shard_map/while/body/concatenate | solution.py:22
  349.6 22.1 %gather_fusion.1 = f32[512,9,3,16]{3,2,1,0:T(4,128)} fusion(f32[4,9,3,16,384]{3,2,4,1,0:T(4,128)} %copy.144, s32[512]{0:T(512)S(1)} %reshape.295), kind=kCustom, calls=%fused_computation.1.clone.clone.1 | custom fusion | bytes 1773568 | tf_op jit(solution)/shard_map/while/body/gather | solution.py:130
  371.8 7.4 %copy.145 = f32[512,9,3,16]{3,0,2,1:T(8,128)} copy(f32[512,9,3,16]{3,2,1,0:T(4,128)} %gather_fusion.1) | data formatting | bytes 1769472 | tf_op jit(solution)/shard_map/while/body/gather | solution.py:130
  379.1 6.7 rev.7
  385.8 7.3 %copy.146 = f32[128,4,9,3,16]{0,2,1,4,3:T(8,128)S(1)} copy(f32[128,4,9,3,16]{4,1,0,3,2:T(4,128)} %rev.7) | data formatting | bytes 1769472 | tf_op jit(solution)/shard_map/while/body/rev | solution.py:130
  423.2 18.7 %copy.144 = f32[4,9,3,16,384]{3,2,4,1,0:T(4,128)} copy(f32[4,9,3,16,384]{4,3,2,1,0:T(8,128)S(1)} %pad_maximum_fusion.2) | data formatting | bytes 5308416 | tf_op jit(solution)/shard_map/while/body/concatenate | solution.py:22
  441.9 22.1 %gather_fusion.1 = f32[512,9,3,16]{3,2,1,0:T(4,128)} fusion(f32[4,9,3,16,384]{3,2,4,1,0:T(4,128)} %copy.144, s32[512]{0:T(512)S(1)} %reshape.295), kind=kCustom, calls=%fused_computation.1.clone.clone.1 | custom fusion | bytes 1773568 | tf_op jit(solution)/shard_map/while/body/gather | solution.py:130
  464.0 7.4 %copy.145 = f32[512,9,3,16]{3,0,2,1:T(8,128)} copy(f32[512,9,3,16]{3,2,1,0:T(4,128)} %gather_fusion.1) | data formatting | bytes 1769472 | tf_op jit(solution)/shard_map/while/body/gather | solution.py:130
  471.4 6.7 rev.7
  478.1 7.3 %copy.146 = f32[128,4,9,3,16]{0,2,1,4,3:T(8,128)S(1)} copy(f32[128,4,9,3,16]{4,1,0,3,2:T(4,128)} %rev.7) | data formatting | bytes 1769472 | tf_op jit(solution)/shard_map/while/body/rev | solution.py:130
  507.4 68.8 %all-to-all-done.2 = f32[81,3,128,16]{0,3,1,2:T(8,128)S(1)} async-done(((f32[81,3,128,16]{0,3,1,2:T(8,128)}), f32[81,3,128,16]{0,3,1,2:T(8,128)S(1)}, u32[]{:S(2)}, u32[]{:S(2)}) %all-to-all-start.2) | async-done | bytes 1990688 | tf_op jit(solution)/shard_map/all_to_all | solution.py:147
  576.8 15.0 %fusion.20 = f32[81,3,4,512]{3,0,2,1:T(8,128)} fusion(f32[81,3,4,512]{0,3,2,1:T(8,128)S(1)} %bitcast.284, f32[512]{0:T(512)S(1)} %compare_select_fusion.3, s32[512]{0:T(512)S(1)} %copy-done.21, pred[512]{0:T(512)(128)(4,1)S(1)} %copy-done.26), kind=kOutput, calls=%fused_computation.35 | convolution fusion | flops 3062104064 | bytes 3985920 | tf_op jit(solution)/shard_map/nser,rz->nsez/dot_general | solution.py:145
  595.1 75.6 %all_to_all.72 = f32[81,3,4,512]{0,2,1,3:T(4,128)S(1)} all-to-all(f32[81,3,4,512]{0,2,1,3:T(4,128)S(1)} %copy.99), channel_id=1, replica_groups=mesh['span'=32,'elem'=8] {'span'}, dimensions={3} | all-to-all | bytes 3981312 | tf_op jit(solution)/shard_map/all_to_all | solution.py:151
  (232 shorter events, 148.1 us)
Async XLA Ops:
  0.0 139.7 %copy-start = (s32[256]{0:T(256)S(1)}, s32[256]{0:T(256)}, u32[]{:S(2)}) copy-start(s32[256]{0:T(256)} %param.20) | copy-start | bytes 3076
  0.0 4.9 copy-start.5
  4.9 4.1 copy-start.11
  17.1 83.1 %all-to-all-start = ((f32[81,3,128,16]{0,3,1,2:T(8,128)}), f32[81,3,128,16]{0,3,1,2:T(8,128)S(1)}, u32[]{:S(2)}, u32[]{:S(2)}) async-start(f32[81,3,128,16]{0,3,1,2:T(8,128)} %copy.73), calls=%async_computation | async-start | bytes 6291456 | tf_op jit(solution)/shard_map/all_to_all | solution.py:100
  29.4 114.1 %copy-start.20 = (s32[512]{0:T(512)}, s32[512]{0:T(512)S(1)}, u32[]{:S(2)}) copy-start(s32[512]{0:T(512)S(1)} %mul.125) | copy-start | bytes 6148
  29.5 71.0 %copy-start.25 = (pred[512]{0:T(512)(128)(4,1)}, pred[512]{0:T(512)(128)(4,1)S(1)}, u32[]{:S(2)}) copy-start(pred[512]{0:T(512)(128)(4,1)S(1)} %eq.42) | copy-start | bytes 1540
  113.0 21.9 %copy-start.12 = (f32[9,9]{1,0:T(8,128)S(1)}, f32[9,9]{1,0:T(8,128)}, u32[]{:S(2)}) copy-start(f32[9,9]{1,0:T(8,128)} %param.19) | copy-start | bytes 976
  113.0 25.4 %copy-start.24 = (f32[9]{0:T(128)S(1)}, f32[9]{0:T(128)}, u32[]{:S(2)}) copy-start(f32[9]{0:T(128)} %param.18) | copy-start | bytes 112
  113.0 25.6 %copy-start.19 = (s32[128,4]{0,1:T(4,128)S(1)}, s32[128,4]{0,1:T(4,128)}, u32[]{:S(2)}) copy-start(s32[128,4]{0,1:T(4,128)} %param.21) | copy-start | bytes 6148
  113.0 93.0 %all-to-all-start.1 = ((f32[81,3,4,512]{0,2,1,3:T(4,128)}), f32[81,3,4,512]{0,2,1,3:T(4,128)S(1)}, u32[]{:S(2)}, u32[]{:S(2)}) async-start(f32[81,3,4,512]{0,2,1,3:T(4,128)} %copy.77), calls=%async_computation.1 | async-start | bytes 6291456 | tf_op jit(solution)/shard_map/all_to_all | solution.py:104
  134.9 4.0 copy-start.23
  134.9 8.6 %copy-start.22 = (f32[3]{0:T(128)S(1)}, f32[3]{0:T(128)}, u32[]{:S(2)}) copy-start(f32[3]{0:T(128)} %param.17) | copy-start | bytes 40
  219.5 5.2 copy-start.3
  220.6 13.1 %collective-permute-start = (f32[4,9,3,16,128]{4,3,2,1,0:T(8,128)S(1)}, f32[4,9,3,16,128]{4,3,2,1,0:T(8,128)}, u32[]{:S(2)}, u32[]{:S(2)}) collective-permute-start(f32[4,9,3,16,128]{4,3,2,1,0:T(8,128)S(1)} %bitcast.271), channel_id=1, source_target_pairs={{1,0},{2,1},{3,2},{4,3},{5,4},{6,5},{7,6},{0,7},{9,8},{10,9},{11,1... | collective-permute-start | bytes 2654216 | tf_op jit(solution)/shard_map/while/body/ppermute | solution.py:21
  223.2 13.8 %collective-permute-start.1 = (f32[4,9,3,16,128]{4,3,2,1,0:T(8,128)S(1)}, f32[4,9,3,16,128]{4,3,2,1,0:T(8,128)}, u32[]{:S(2)}, u32[]{:S(2)}) collective-permute-start(f32[4,9,3,16,128]{4,3,2,1,0:T(8,128)S(1)} %bitcast.272), channel_id=1, source_target_pairs={{0,1},{1,2},{2,3},{3,4},{4,5},{5,6},{6,7},{7,0},{8,9},{9,10},{10,1... | collective-permute-start | bytes 2654216 | tf_op jit(solution)/shard_map/while/body/ppermute | solution.py:18
  293.6 7.3 %copy-start.13 = (f32[4,9,81,1,1]{2,1,0,4,3:T(8,128)S(1)}, f32[4,9,81,1,1]{2,1,0,4,3:T(8,128)}, u32[]{:S(2)}) copy-start(f32[4,9,81,1,1]{2,1,0,4,3:T(8,128)} %get-tuple-element.298) | copy-start | bytes 34996 | tf_op jit(solution)/shard_map/while
  315.4 10.6 %collective-permute-start = (f32[4,9,3,16,128]{4,3,2,1,0:T(8,128)S(1)}, f32[4,9,3,16,128]{4,3,2,1,0:T(8,128)}, u32[]{:S(2)}, u32[]{:S(2)}) collective-permute-start(f32[4,9,3,16,128]{4,3,2,1,0:T(8,128)S(1)} %bitcast.271), channel_id=1, source_target_pairs={{1,0},{2,1},{3,2},{4,3},{5,4},{6,5},{7,6},{0,7},{9,8},{10,9},{11,1... | collective-permute-start | bytes 2654216 | tf_op jit(solution)/shard_map/while/body/ppermute | solution.py:21
  315.4 13.8 %collective-permute-start.1 = (f32[4,9,3,16,128]{4,3,2,1,0:T(8,128)S(1)}, f32[4,9,3,16,128]{4,3,2,1,0:T(8,128)}, u32[]{:S(2)}, u32[]{:S(2)}) collective-permute-start(f32[4,9,3,16,128]{4,3,2,1,0:T(8,128)S(1)} %bitcast.272), channel_id=1, source_target_pairs={{0,1},{1,2},{2,3},{3,4},{4,5},{5,6},{6,7},{7,0},{8,9},{9,10},{10,1... | collective-permute-start | bytes 2654216 | tf_op jit(solution)/shard_map/while/body/ppermute | solution.py:18
  385.8 7.3 %copy-start.13 = (f32[4,9,81,1,1]{2,1,0,4,3:T(8,128)S(1)}, f32[4,9,81,1,1]{2,1,0,4,3:T(8,128)}, u32[]{:S(2)}) copy-start(f32[4,9,81,1,1]{2,1,0,4,3:T(8,128)} %get-tuple-element.298) | copy-start | bytes 34996 | tf_op jit(solution)/shard_map/while
  407.6 10.6 %collective-permute-start = (f32[4,9,3,16,128]{4,3,2,1,0:T(8,128)S(1)}, f32[4,9,3,16,128]{4,3,2,1,0:T(8,128)}, u32[]{:S(2)}, u32[]{:S(2)}) collective-permute-start(f32[4,9,3,16,128]{4,3,2,1,0:T(8,128)S(1)} %bitcast.271), channel_id=1, source_target_pairs={{1,0},{2,1},{3,2},{4,3},{5,4},{6,5},{7,6},{0,7},{9,8},{10,9},{11,1... | collective-permute-start | bytes 2654216 | tf_op jit(solution)/shard_map/while/body/ppermute | solution.py:21
  407.7 13.8 %collective-permute-start.1 = (f32[4,9,3,16,128]{4,3,2,1,0:T(8,128)S(1)}, f32[4,9,3,16,128]{4,3,2,1,0:T(8,128)}, u32[]{:S(2)}, u32[]{:S(2)}) collective-permute-start(f32[4,9,3,16,128]{4,3,2,1,0:T(8,128)S(1)} %bitcast.272), channel_id=1, source_target_pairs={{0,1},{1,2},{2,3},{3,4},{4,5},{5,6},{6,7},{7,0},{8,9},{9,10},{10,1... | collective-permute-start | bytes 2654216 | tf_op jit(solution)/shard_map/while/body/ppermute | solution.py:18
  478.1 7.3 %copy-start.13 = (f32[4,9,81,1,1]{2,1,0,4,3:T(8,128)S(1)}, f32[4,9,81,1,1]{2,1,0,4,3:T(8,128)}, u32[]{:S(2)}) copy-start(f32[4,9,81,1,1]{2,1,0,4,3:T(8,128)} %get-tuple-element.298) | copy-start | bytes 34996 | tf_op jit(solution)/shard_map/while
  501.2 6.1 copy-start.21
  501.2 75.0 %all-to-all-start.2 = ((f32[81,3,128,16]{0,3,1,2:T(8,128)}), f32[81,3,128,16]{0,3,1,2:T(8,128)S(1)}, u32[]{:S(2)}, u32[]{:S(2)}) async-start(f32[81,3,128,16]{0,3,1,2:T(8,128)} %bitcast.278), calls=%async_computation.2 | async-start | bytes 6291456 | tf_op jit(solution)/shard_map/all_to_all | solution.py:147
  (38 other events, 46.1 us)
where the time goes:
time: 682 us; the launch traced here: 674 us
  local copies, waits for them, and re-layouts  246 us (36%)
  waiting for transfers between devices  226 us (33%)
  blocking collectives  75.6 us (11%)
  matrix products  53.9 us (8%)
  starting transfers between devices  43.6 us (6%)
  other arithmetic  25 us (4%)
    gather x6, local copies, waits for them, and re-layouts, couple(): across = gather_pool(traces)[edge_map, :, :, :, position][:, :, ::-1]  88.5 us
    all_to_all x1, blocking collectives, body(): lax.all_to_all(values, 'span', split_axis=3, concat_axis=2, tiled=True)  75.6 us
    all_to_all x1, waiting for transfers between devices, body(): lax.all_to_all(source_swapped, 'span', split_axis=2, concat_axis=3, tiled...  70.7 us
    all_to_all x1, waiting for transfers between devices, body(): lax.all_to_all(solution_swapped, 'span', split_axis=2, concat_axis=3, til...  68.8 us
    all_to_all x1, waiting for transfers between devices, body(): lax.all_to_all(coeffs, 'span', split_axis=3, concat_axis=2, tiled=True)  61.5 us
    concatenate x3, local copies, waits for them, and re-layouts, extended(): block = jnp.concatenate([low, block, high], axis=dim)  56.2 us
    rev x6, local copies, waits for them, and re-layouts, couple(): across = gather_pool(traces)[edge_map, :, :, :, position][:, :, ::-1]  42 us
    all_to_all x1, starting transfers between devices, body(): lax.all_to_all(coeffs, 'span', split_axis=3, concat_axis=2, tiled=True)  21.9 us
  transfers between devices with their start and end apart: 9, of which 9 were waited for; matrix products, arithmetic and copies ran while one was open for 4% of the time, Pallas kernels for 0%

commit v1 on v0

v1 whole, which is shorter than its diff:
```python
import functools

import jax
import jax.numpy as jnp
import numpy as np
from jax import lax
from jax.experimental import pallas as pl
from jax.experimental.pallas import tpu as pltpu
from jax.sharding import PartitionSpec as P

MESH_X = 16
PER_SIDE = 9
SPECIES = 3
NS = PER_SIDE * PER_SIDE * SPECIES
LANES = 256
COUPLING = 0.2
SWEEPS = 3
GROUPS = 2
F32 = jnp.float32
BF16 = jnp.bfloat16
HIGHEST = lax.Precision.HIGHEST
MESH = pl.DeviceIdType.MESH
SOUTH, EAST, NORTH, WEST = 0, 1, 2, 3
VMEM_LIMIT = 60 * 1024 * 1024

NN_DIMS = (((1,), (0,)), ((), ()))
NT_DIMS = (((1,), (1,)), ((), ()))
TN_DIMS = (((0,), (0,)), ((), ()))


def split(x):
    high = x.astype(BF16)
    return high, (x - high.astype(F32)).astype(BF16)


def dot(a, b, dims=NN_DIMS):
    return lax.dot_general(a, b, dims, preferred_element_type=F32)


def dot3(a, b, dims=NN_DIMS):
    return dot(a[0], b[0], dims) + dot(a[0], b[1], dims) + dot(a[1], b[0], dims)


def edge_lists():
    last = PER_SIDE - 1
    return [
        [i for i in range(PER_SIDE)],
        [i * PER_SIDE + last for i in range(PER_SIDE)],
        [last * PER_SIDE + last - i for i in range(PER_SIDE)],
        [(last - i) * PER_SIDE for i in range(PER_SIDE)],
    ]


def selection_tables():
    pair_i = np.zeros((LANES, PER_SIDE), np.float32)
    pair_j = np.zeros((LANES, PER_SIDE), np.float32)
    pair_s = np.full((LANES,), -1)
    for lane in range(NS):
        node, s = divmod(lane, SPECIES)
        pair_i[lane, node // PER_SIDE] = 1.0
        pair_j[lane, node % PER_SIDE] = 1.0
        pair_s[lane] = s
    out_i = np.zeros((4, 128, PER_SIDE), np.float32)
    out_j = np.zeros((4, 128, PER_SIDE), np.float32)
    in_i = np.zeros((4, 128, PER_SIDE), np.float32)
    in_j = np.zeros((4, 128, PER_SIDE), np.float32)
    trace_s = np.full((128,), -2)
    edges = edge_lists()
    for rotation in range(4):
        for d in range(4):
            nodes = edges[(rotation + d) % 4]
            for t in range(PER_SIDE):
                for s in range(SPECIES):
                    lane = d * 32 + t * SPECIES + s
                    trace_s[lane] = s
                    out_i[rotation, lane, nodes[t] // PER_SIDE] = 1.0
                    out_j[rotation, lane, nodes[t] % PER_SIDE] = 1.0
                    back = nodes[PER_SIDE - 1 - t]
                    in_i[rotation, lane, back // PER_SIDE] = 1.0
                    in_j[rotation, lane, back % PER_SIDE] = 1.0
    pair_mask = (pair_s[:, None] == pair_s[None, :]) & (pair_s[:, None] >= 0)
    trace_mask = trace_s[:, None] == pair_s[None, :]
    return dict(
        pair_i=pair_i,
        pair_j=pair_j,
        edges=np.stack([out_i, out_j, in_i, in_j], axis=1).reshape(4, -1),
        pair_mask=pair_mask.astype(np.float32),
        trace_mask=np.tile(trace_mask.astype(np.float32), (4, 1)),
    )


def transform_tables(planes):
    modes = planes // 2
    phase = (np.arange(modes)[:, None] * np.arange(planes)[None, :]) % planes
    angle = phase.astype(np.float64) * (2.0 * np.pi / planes)
    trig = np.concatenate([np.cos(angle), -np.sin(angle)], axis=0)
    weight = np.where(np.arange(modes) == 0, 1.0, 2.0)
    weight = np.concatenate([weight, weight])
    return np.float32(trig / planes), np.float32((trig * weight[:, None]).T)


def split_table(table):
    high = table.astype(BF16)
    low = (table - high.astype(np.float32)).astype(BF16)
    return jnp.asarray(high), jnp.asarray(low)


def order_kernel(n_span, n_elem, own, cols, table_ref, place_ref, turn_ref):
    me = lax.axis_index("elem")
    rows = own // cols
    block_rows = rows // 2
    odd = lax.rem(me, 2)
    start = table_ref[4 * own]
    dart = lax.fori_loop(0, rows * me, lambda i, d: table_ref[d], start)
    norths = []
    for row in range(rows):
        norths.append(dart)
        if row + 1 < rows:
            dart = table_ref[dart]
    easts = []
    for dart in norths:
        edge = dart // own % 8
        easts.append(dart + ((edge + 3) % 4 - edge) * own)
    lane = lax.broadcasted_iota(jnp.int32, (1, own), 1)
    for col in range(cols):
        for row in range(rows):
            dart = easts[row]
            block_row = row // 2
            x = jnp.where(odd == 1, block_rows - 1 - block_row, block_row)
            slot = (row % 2 * 2 + col % 2) * n_span + (col // 2) * block_rows + x
            local = dart % own
            edge = dart // own % 8
            turn_ref[slot] = (edge + 3) % 4
            place_ref[pl.ds(slot, 1), :] = (lane == local).astype(F32)
            if col + 1 < cols:
                easts[row] = table_ref[dart]


def source_kernel(
    n_span, depth, own, species_ref, laplacian_ref, binary_ref, dref_ref, place_ref, out_ref, source_ref
):
    nodes = PER_SIDE * PER_SIDE
    inverse = [[1.0 / binary_ref[s, j] for j in range(SPECIES + 1)] for s in range(SPECIES)]
    dref = [dref_ref[s] for s in range(SPECIES)]
    over = [1.0 / dref_ref[s] for s in range(SPECIES)]
    source_ref[pl.ds(NS * depth, (LANES - NS) * depth), :] = jnp.zeros(((LANES - NS) * depth, own), F32)

    def one_node(node, carry):
        base = pl.multiple_of(node * SPECIES * depth, 8)
        parts = [species_ref[pl.ds(base + s * depth, depth), :] for s in range(SPECIES)]
        slopes = [laplacian_ref[pl.ds(base + s * depth, depth), :] for s in range(SPECIES)]
        bath = 1.0 - (parts[0] + parts[1] + parts[2])
        for s in range(SPECIES):
            resistance = bath * inverse[s][SPECIES]
            for j in range(SPECIES):
                if j != s:
                    resistance = resistance + parts[j] * inverse[s][j]
            mixture = (1.0 - parts[s]) / resistance
            value = (parts[s] + (mixture - dref[s]) * slopes[s]) * over[s]
            source_ref[pl.ds(base + s * depth, depth), :] = value
        return carry

    lax.fori_loop(0, nodes, one_node, 0, unroll=3)
    place = place_ref[...].astype(BF16)
    for plane in range(depth):
        high, low = split(source_ref[pl.ds(plane, LANES, stride=depth), :])
        moved = dot(place, high, NT_DIMS) + dot(place, low, NT_DIMS)
        for e in range(4):
            for h in range(2):
                out_ref[pl.ds((e * 2 + h) * depth + plane, n_span, stride=8 * depth), :] = moved[
                    e * n_span : (e + 1) * n_span, h * 128 : (h + 1) * 128
                ]


def finish_kernel(n_span, depth, own, values_ref, place_ref, out_ref):
    place = place_ref[...].astype(BF16)
    for plane in range(depth):
        for h in range(2):
            parts = [
                values_ref[pl.ds((e * 2 + h) * depth + plane, n_span, stride=8 * depth), :]
                for e in range(4)
            ]
            high, low = split(jnp.concatenate(parts, axis=0))
            moved = dot(high, place, TN_DIMS) + dot(low, place, TN_DIMS)
            count = min(NS - h * 128, 128)
            out_ref[pl.ds(h * 128 * depth + plane, count, stride=depth), :] = moved[:count]


def neighbours(n_span, n_elem, block_rows):
    span, elem = lax.axis_index("span"), lax.axis_index("elem")
    x = span % block_rows
    odd = elem % 2
    up = 1 - 2 * odd
    block_row = jnp.where(odd == 1, block_rows - 1 - x, x)
    last, first = block_row == block_rows - 1, block_row == 0
    return {
        NORTH: (jnp.where(last, span, span + up), jnp.where(last, (elem + 1) % n_elem, elem)),
        SOUTH: (jnp.where(first, span, span - up), jnp.where(first, (elem + n_elem - 1) % n_elem, elem)),
        EAST: ((span + block_rows) % n_span, elem),
        WEST: ((span + n_span - block_rows) % n_span, elem),
    }


def solve_kernel(
    n_span,
    n_elem,
    planes,
    block_rows,
    values_ref,
    forward_high,
    forward_low,
    backward_high,
    backward_low,
    pair_ref,
    out_trace_ref,
    in_trace_ref,
    diag_ref,
    rounds_ref,
    result_ref,
    work_high,
    work_low,
    rhs_ref,
    modal_ref,
    inverse_ref,
    trace_ref,
    send_ref,
    recv_ref,
    send_sem,
    recv_sem,
):
    modes = planes // 2
    depth = planes // n_span
    group = planes // GROUPS
    half = group // 2
    tile = min(256, planes)
    near = neighbours(n_span, n_elem, block_rows)
    barrier = pltpu.get_barrier_semaphore()
    for d in range(4):
        pl.semaphore_signal(barrier, inc=1, device_id=near[d], device_id_type=MESH)

    row = lax.broadcasted_iota(jnp.int32, (planes, LANES), 0)
    mode = jnp.where(row >= modes, row - modes, row).astype(F32)
    wave = mode * (8.0 / planes)
    inverse_ref[...] = 1.0 / (wave * wave + diag_ref[...])

    pair = split(pair_ref[...])

    for e in range(4):
        for start in range(0, planes, tile):
            rows = pl.ds(start, tile)
            blocks = pl.ds(start // depth, tile // depth)
            halves = [values_ref[blocks, e * 2 + h].reshape(tile, 128) for h in range(2)]
            high, low = split(dot3(split(jnp.concatenate(halves, axis=1)), pair))
            work_high[rows, pl.ds(e * LANES, LANES)] = high
            work_low[rows, pl.ds(e * LANES, LANES)] = low

    def to_modes(step, carry):
        rows = pl.ds(pl.multiple_of(step * tile, tile), tile)
        table = forward_high[rows, :], forward_low[rows, :]
        scale = inverse_ref[rows, :]
        for e in range(4):
            cols = pl.ds(e * LANES, LANES)
            rhs = dot3(table, (work_high[:, cols], work_low[:, cols]))
            rhs_ref[e, rows, :] = rhs
            modal_ref[e, rows, :] = rhs * scale
        return carry

    lax.fori_loop(0, planes // tile, to_modes, 0)

    to_trace = [split(out_trace_ref[pl.ds(e * 128, 128), :]) for e in range(4)]
    from_trace = [split(in_trace_ref[pl.ds(e * 128, 128), :]) for e in range(4)]
    lane_group = lax.broadcasted_iota(jnp.int32, (1, 128), 1) // 32
    outer = {NORTH: (2, 3), SOUTH: (0, 1), EAST: (1, 3), WEST: (0, 2)}

    def copies(sweep, g):
        opposite = {NORTH: SOUTH, SOUTH: NORTH, EAST: WEST, WEST: EAST}
        return [
            pltpu.make_async_remote_copy(
                src_ref=send_ref.at[sweep, g, d],
                dst_ref=recv_ref.at[sweep, g, opposite[d]],
                send_sem=send_sem.at[sweep, g, d],
                recv_sem=recv_sem.at[sweep, g, opposite[d]],
                device_id=near[d],
                device_id_type=MESH,
            )
            for d in range(4)
        ]

    def send_traces(sweep, g):
        rows = pl.ds(g * group, group)
        traces = []
        for e in range(4):
            trace = dot3(split(modal_ref[e, rows, :]), to_trace[e], NT_DIMS)
            trace_ref[e, rows, :] = trace
            traces.append(trace)
        for d in range(4):
            packed = None
            for h in range(2):
                for q in range(2):
                    piece = traces[outer[d][q]][h * half : (h + 1) * half]
                    goal = h * 2 + q
                    shift = (goal - d) % 4 * 32
                    if shift:
                        piece = pltpu.roll(piece, shift, 1)
                    packed = piece if packed is None else jnp.where(lane_group == goal, piece, packed)
            send_ref[sweep, g, d] = packed
        for copy in copies(sweep, g):
            copy.start()

    def update(sweep, g):
        for copy in copies(sweep, g):
            copy.wait_recv()
        for h in range(2):
            rows = pl.ds(g * group + h * half, half)
            active = rounds_ref[rows, :] > sweep + 1
            active = jnp.concatenate([active, active], axis=1)
            scale = inverse_ref[rows, :]
            for e in range(4):
                a, b = divmod(e, 2)
                across = None
                sides = (
                    (NORTH, None) if a == 0 else (NORTH, b),
                    (SOUTH, b) if a == 0 else (SOUTH, None),
                    (EAST, None) if b == 0 else (EAST, a),
                    (WEST, a) if b == 0 else (WEST, None),
                )
                for d, q in sides:
                    if q is None:
                        other = (2 * (1 - a) + b) if d in (NORTH, SOUTH) else (2 * a + 1 - b)
                        piece = pltpu.roll(trace_ref[other, rows, :], 64, 1)
                    else:
                        piece = recv_ref[sweep, g, d]
                        shift = (d - (h * 2 + q)) % 4 * 32
                        if shift:
                            piece = pltpu.roll(piece, shift, 1)
                    across = piece if across is None else jnp.where(lane_group == d, piece, across)
                fresh = (rhs_ref[e, rows, :] + dot3(split(across), from_trace[e])) * scale
                modal_ref[e, rows, :] = jnp.where(active, fresh, modal_ref[e, rows, :])

    pl.semaphore_wait(barrier, 4)
    for g in range(GROUPS):
        send_traces(0, g)
    for sweep in range(SWEEPS):
        for g in range(GROUPS):
            update(sweep, g)
            if sweep + 1 < SWEEPS:
                send_traces(sweep + 1, g)

    for e in range(4):
        for start in range(0, planes, tile):
            rows = pl.ds(start, tile)
            high, low = split(dot3(split(modal_ref[e, rows, :]), pair, NT_DIMS))
            work_high[rows, pl.ds(e * LANES, LANES)] = high
            work_low[rows, pl.ds(e * LANES, LANES)] = low

    def to_planes(step, carry):
        rows = pl.ds(pl.multiple_of(step * tile, tile), tile)
        table = backward_high[rows, :], backward_low[rows, :]
        for e in range(4):
            cols = pl.ds(e * LANES, LANES)
            value = dot3(table, (work_high[:, cols], work_low[:, cols]))
            for h in range(2):
                part = value[:, h * 128 : (h + 1) * 128]
                result_ref[pl.ds(step * (tile // depth), tile // depth), e * 2 + h] = part.reshape(
                    tile // depth, depth, 128
                )
        return carry

    lax.fori_loop(0, planes // tile, to_planes, 0)
    for sweep in range(SWEEPS):
        for g in range(GROUPS):
            for copy in copies(sweep, g):
                copy.wait_send()


def vmem():
    return pl.BlockSpec(memory_space=pltpu.VMEM)


def smem():
    return pl.BlockSpec(memory_space=pltpu.SMEM)


def body(species, laplacian, binary, dref, stiff_eig, basis, rounds, adjacency, edge_map):
    n_span = lax.axis_size("span")
    n_elem = lax.axis_size("elem")
    depth = species.shape[2]
    own = species.shape[3]
    planes = depth * n_span
    cols = MESH_X
    block_rows = own // cols // 2
    tables = selection_tables()

    ahead_id, ahead_edge = adjacency.T, edge_map.T
    owner = ahead_id // own
    step = owner * (8 * own) + (ahead_edge + 2) % 4 * own + ahead_id % own
    before = (lax.axis_index("elem") + n_elem - 1) % n_elem
    edge_ids = lax.broadcasted_iota(jnp.int32, (4, own), 0)
    elem_ids = lax.broadcasted_iota(jnp.int32, (4, own), 1)
    facing = jnp.where(owner == before, (edge_ids + 2) % 4 * own + elem_ids, 8 * own)
    start = jnp.broadcast_to(jnp.min(facing), (4, own))
    local_table = jnp.concatenate([step, start], axis=0)
    table = lax.all_to_all(
        jnp.broadcast_to(local_table[None], (n_elem, 8, own)), "elem", split_axis=0, concat_axis=0, tiled=True
    ).reshape(n_elem * 8 * own)

    place, turn = pl.pallas_call(
        functools.partial(order_kernel, n_span, n_elem, own, cols),
        out_shape=(
            jax.ShapeDtypeStruct((own, own), F32),
            jax.ShapeDtypeStruct((own,), jnp.int32),
        ),
        in_specs=[smem()],
        out_specs=(vmem(), smem()),
        name="order",
    )(table)

    sent = pl.pallas_call(
        functools.partial(source_kernel, n_span, depth, own),
        out_shape=jax.ShapeDtypeStruct((n_span * 8 * depth, 128), F32),
        in_specs=[vmem(), vmem(), smem(), smem(), vmem()],
        out_specs=vmem(),
        scratch_shapes=[pltpu.VMEM((LANES * depth, own), F32)],
        compiler_params=pltpu.CompilerParams(vmem_limit_bytes=VMEM_LIMIT),
        name="source",
    )(
        species.reshape(NS * depth, own),
        laplacian.reshape(NS * depth, own),
        binary,
        dref,
        place,
    )
    gathered = lax.all_to_all(
        sent.reshape(n_span, 8, depth, 128), "span", split_axis=0, concat_axis=0, tiled=True
    )

    def spread(left_i, left_j, matrix, right_i, right_j):
        one = jnp.dot(jnp.dot(left_i, matrix, precision=HIGHEST), right_i.T, precision=HIGHEST)
        two = jnp.dot(jnp.dot(left_j, matrix, precision=HIGHEST), right_j.T, precision=HIGHEST)
        return one * two

    pair = spread(tables["pair_i"], tables["pair_j"], basis, tables["pair_i"], tables["pair_j"])
    pair = pair * tables["pair_mask"]
    my_turn = lax.dynamic_slice_in_dim(turn.reshape(4, n_span), lax.axis_index("span"), 1, axis=1)
    chosen = (my_turn == jnp.arange(4)[None, :]).astype(F32)
    edges = jnp.dot(chosen, tables["edges"]).reshape(4, 4, 128, PER_SIDE)
    out_i, out_j, in_i, in_j = [edges[:, i].reshape(512, PER_SIDE) for i in range(4)]
    out_trace = spread(out_i, out_j, basis, tables["pair_i"], tables["pair_j"])
    out_trace = out_trace * tables["trace_mask"]
    in_trace = spread(in_i, in_j, basis, tables["pair_i"], tables["pair_j"])
    in_trace = in_trace * (COUPLING * tables["trace_mask"])
    eig_sum = (stiff_eig[:, None] + stiff_eig[None, :]).reshape(-1)
    diag = (eig_sum[:, None] + 1.0 / dref[None, :]).reshape(1, NS)
    diag = jnp.pad(diag, ((0, 0), (0, LANES - NS)), constant_values=1.0)
    row_rounds = jnp.broadcast_to(jnp.concatenate([rounds, rounds])[:, None], (planes, 128))
    forward, backward = transform_tables(planes)

    group = planes // GROUPS
    halo = (SWEEPS, GROUPS, 4, group // 2, 128)
    solved = pl.pallas_call(
        functools.partial(solve_kernel, n_span, n_elem, planes, block_rows),
        out_shape=jax.ShapeDtypeStruct((n_span, 8, depth, 128), F32),
        in_specs=[vmem()] * 10,
        out_specs=vmem(),
        scratch_shapes=[
            pltpu.VMEM((planes, 4 * LANES), BF16),
            pltpu.VMEM((planes, 4 * LANES), BF16),
            pltpu.VMEM((4, planes, LANES), F32),
            pltpu.VMEM((4, planes, LANES), F32),
            pltpu.VMEM((planes, LANES), F32),
            pltpu.VMEM((4, planes, 128), F32),
            pltpu.VMEM(halo, F32),
            pltpu.VMEM(halo, F32),
            pltpu.SemaphoreType.DMA(halo[:3]),
            pltpu.SemaphoreType.DMA(halo[:3]),
        ],
        compiler_params=pltpu.CompilerParams(
            collective_id=0, has_side_effects=True, vmem_limit_bytes=VMEM_LIMIT
        ),
        name="solve",
    )(
        gathered,
        *split_table(forward),
        *split_table(backward),
        pair,
        out_trace,
        in_trace,
        diag,
        row_rounds,
    )
    returned = lax.all_to_all(solved, "span", split_axis=0, concat_axis=0, tiled=True)
    updated = pl.pallas_call(
        functools.partial(finish_kernel, n_span, depth, own),
        out_shape=jax.ShapeDtypeStruct((NS * depth, own), F32),
        in_specs=[vmem(), vmem()],
        out_specs=vmem(),
        compiler_params=pltpu.CompilerParams(vmem_limit_bytes=VMEM_LIMIT),
        name="finish",
    )(returned.reshape(n_span * 8 * depth, 128), place)
    return updated.reshape(species.shape)


def solution(mesh):
    return jax.shard_map(
        body,
        mesh=mesh,
        in_specs=(
            P(None, None, "span", "elem"),
            P(None, None, "span", "elem"),
            P(),
            P(),
            P(),
            P(),
            P(),
            P("elem", None),
            P("elem", None),
        ),
        out_specs=P(None, None, "span", "elem"),
        check_vma=False,
    )
```

time: 682 us -> 174 us (0.26); the launches traced: 674 us -> 173 us
  local copies, waits for them, and re-layouts: 246 us -> 4.25 us
  waiting for transfers between devices: 226 us -> 40 us
  matrix products: 53.9 us -> 7.27 us
  Pallas kernels: 0 us -> 42.7 us
  starting transfers between devices: 43.6 us -> 11.7 us
  other arithmetic: 25 us -> 1.58 us
  blocking collectives: 75.6 us -> 65.3 us
    all_to_all x3 -> x1, waiting for transfers between devices: 201 us -> 40 us  [body(): lax.all_to_all(sent.reshape(n_span, 8, depth, 128), 'span', split_axis=0,...]
    gather x11 -> x0, local copies, waits for them, and re-layouts: 93.4 us -> none  [the longest x6 88.5 us: couple(): across = gather_pool(traces)[edge_map, :, :, :, position][:, :, ::-1]]
    concatenate x6 -> x1, local copies, waits for them, and re-layouts: 56.5 us -> 0.65 us  [body(): local_table = jnp.concatenate([step, start], axis=0)]
    dot_general x13, matrix products: 53.9 us -> 7.27 us  [the longest x3 3.78 us: spread(): jnp.dot(jnp.dot(left_j, matrix, precision=HIGHEST), right_j.T, precision=...]
    pallas_call x0 -> x4, Pallas kernels: none -> 42.7 us  [the longest x1 27.5 us: body(): pl.pallas_call(functools.partial(solve_kernel, n_span, n_elem, planes, bl...]
    rev x6 -> x0, local copies, waits for them, and re-layouts: 42 us -> none  [couple(): across = gather_pool(traces)[edge_map, :, :, :, position][:, :, ::-1]]
    all_to_all x3 -> x1, starting transfers between devices: 40 us -> 11.7 us  [body(): lax.all_to_all(sent.reshape(n_span, 8, depth, 128), 'span', split_axis=0,...]
    ppermute x6 -> x0, waiting for transfers between devices: 24.8 us -> none  [the longest x3 15.1 us: extended(): lax.ppermute(lax.slice_in_dim(block, 0, width, axis=dim), axis, backward)]
  transfers between devices with their start and end apart: 9 -> 1, of which waited for: 9 -> 1; matrix products, arithmetic and copies ran while one was open for 4% -> 6% of each run, Pallas kernels for 0% -> 0%
where the time goes in v1:
time: 174 us; the launch traced here: 173 us
  blocking collectives  65.3 us (38%)
  Pallas kernels  42.7 us (25%)
  waiting for transfers between devices  40 us (23%)
  starting transfers between devices  11.7 us (7%)
  matrix products  7.27 us (4%)
  local copies, waits for them, and re-layouts  4.25 us (2%)
    all_to_all x1, blocking collectives, body(): lax.all_to_all(solved, 'span', split_axis=0, concat_axis=0, tiled=True)  55.5 us
    all_to_all x1, waiting for transfers between devices, body(): lax.all_to_all(sent.reshape(n_span, 8, depth, 128), 'span', split_axis=0,...  40 us
    pallas_call x1, Pallas kernels, body(): pl.pallas_call(functools.partial(solve_kernel, n_span, n_elem, planes, bl...  27.5 us
    all_to_all x1, starting transfers between devices, body(): lax.all_to_all(sent.reshape(n_span, 8, depth, 128), 'span', split_axis=0,...  11.7 us
    all_to_all x1, blocking collectives, body(): lax.all_to_all(jnp.broadcast_to(local_table[None], (n_elem, 8, own)), 'el...  9.82 us
    pallas_call x1, Pallas kernels, body(): pl.pallas_call(functools.partial(source_kernel, n_span, depth, own), out_...  6.7 us
    pallas_call x1, Pallas kernels, body(): pl.pallas_call(functools.partial(finish_kernel, n_span, depth, own), out_...  5.14 us
    dot_general x3, matrix products, spread(): jnp.dot(jnp.dot(left_j, matrix, precision=HIGHEST), right_j.T, precision=...  3.78 us
  transfers between devices with their start and end apart: 1, of which 1 were waited for; matrix products, arithmetic and copies ran while one was open for 6% of the time, Pallas kernels for 0%

profile of v1, /device:TPU:6, one launch (start us, length us, event | category | flops | bytes accessed | tf_op | source)
XLA Modules:
  0.0 173.1 jit_solution(13451953461725441710)
XLA Ops:
  0.0 1.4 select_reduce_fusion
  1.4 0.6 concatenate.6
  2.1 9.8 %all_to_all.15 = s32[8,8,128]{2,1,0:T(8,128)} all-to-all(s32[8,8,128]{2,1,0:T(8,128)S(1)} %broadcast_in_dim.6), channel_id=1, replica_groups=mesh['span'=32,'elem'=8] {'elem'}, dimensions={0} | all-to-all | bytes 65536 | tf_op jit(solution)/shard_map/all_to_all | solution.py:403
  11.9 3.3 %order.1 = (f32[128,128]{1,0:T(8,128)}, s32[128]{0:T(128)}) custom-call(s32[8192]{0:T(1024)} %bitcast.73), custom_call_target="tpu_custom_call" | custom-call | tf_op jit(solution)/shard_map/order/pallas_call | solution.py:407
  15.2 6.7 %source.1 = f32[4096,128]{1,0:T(8,128)} custom-call(f32[3888,128]{1,0:T(8,128)} %bitcast.67, f32[3888,128]{1,0:T(8,128)} %bitcast.68, f32[3,4]{1,0:T(4,128)} %binary_ref.1, f32[3]{0:T(128)} %dref_ref.1, f32[128,128]{1,0:T(8,128)} %get-tuple-element.7.place_ref), custom_call_target="tpu_custom_call" | custom-call | tf_op jit(solution)/shard_map/source/pallas_call | solution.py:418
  22.0 11.7 %all-to-all-start.1 = ((f32[32,8,16,128]{3,2,1,0:T(8,128)}), f32[32,8,16,128]{3,2,1,0:T(8,128)S(1)}, u32[]{:S(2)}, u32[]{:S(2)}) async-start(f32[32,8,16,128]{3,2,1,0:T(8,128)} %bitcast.65), calls=%async_computation.1 | async-start | bytes 4194304 | tf_op jit(solution)/shard_map/all_to_all | solution.py:433
  34.2 0.6 pad.5.diag_ref
  35.3 0.3 fusion.14
  35.7 1.1 fusion.2.pair_ref
  37.2 1.0 reshape.72
  38.3 0.3 fusion.16
  38.6 0.3 fusion.18
  39.0 0.3 fusion.19
  39.3 0.3 fusion.21
  39.7 0.5 fusion.17
  40.2 0.6 fusion.20
  40.8 1.3 fusion.out_trace_ref
  42.2 1.4 fusion.1.in_trace_ref
  43.5 40.0 %all-to-all-done.1.values_ref = f32[32,8,16,128]{3,2,1,0:T(8,128)S(1)} async-done(((f32[32,8,16,128]{3,2,1,0:T(8,128)}), f32[32,8,16,128]{3,2,1,0:T(8,128)S(1)}, u32[]{:S(2)}, u32[]{:S(2)}) %all-to-all-start.1) | async-done | bytes 2097184 | tf_op jit(solution)/shard_map/all_to_all | solution.py:433
  83.5 1.0 broadcast_in_dim.7.rounds_ref
  84.5 0.4 copy-done.1
  84.9 27.5 %solve.1 = f32[32,8,16,128]{3,2,1,0:T(8,128)} custom-call(f32[32,8,16,128]{3,2,1,0:T(8,128)} %copy-done.1, bf16[512,512]{1,0:T(8,128)(2,1)} %constant.113.clone.forward_high, bf16[512,512]{1,0:T(8,128)(2,1)} %constant.114.clone.forward_low, bf16[512,512]{1,0:T(8,128)(2,1)} %constant.115.clone.backward_high, bf16[512,512]{1,0:T(8,128)(2,1)} %constant.116.clone.backward_low, ...), custom_call_target="tpu_custom_call" | custom-call | tf_op jit(solution)/shard_map/solve/pallas_call | solution.py:460
  112.5 55.5 %all_to_all.16 = f32[32,8,16,128]{3,2,1,0:T(8,128)} all-to-all(f32[32,8,16,128]{3,2,1,0:T(8,128)} %solve.1), channel_id=1, replica_groups=mesh['span'=32,'elem'=8] {'span'}, dimensions={0} | all-to-all | bytes 4194304 | tf_op jit(solution)/shard_map/all_to_all | solution.py:491
  168.0 5.1 %finish.1 = f32[3888,128]{1,0:T(8,128)} custom-call(f32[4096,128]{1,0:T(8,128)} %bitcast.66, f32[128,128]{1,0:T(8,128)} %get-tuple-element.7.place_ref), custom_call_target="tpu_custom_call" | custom-call | tf_op jit(solution)/shard_map/finish/pallas_call | solution.py:492
  (42 shorter events, 1.5 us)
Async XLA Ops:
  0.0 34.8 %copy-start = (f32[9,9]{1,0:T(8,128)S(1)}, f32[9,9]{1,0:T(8,128)}, u32[]{:S(2)}) copy-start(f32[9,9]{1,0:T(8,128)} %param.30) | copy-start | bytes 976
  21.9 11.8 %copy-start.10 = (f32[9]{0:T(128)S(1)}, f32[9]{0:T(128)}, u32[]{:S(2)}) copy-start(f32[9]{0:T(128)} %param.29) | copy-start | bytes 112
  21.9 12.0 %copy-start.12 = (f32[3]{0:T(128)S(1)}, f32[3]{0:T(128)}, u32[]{:S(2)}) copy-start(f32[3]{0:T(128)} %dref_ref.1) | copy-start | bytes 40
  21.9 12.8 %copy-start.11 = (s32[256]{0:T(256)S(1)}, s32[256]{0:T(256)}, u32[]{:S(2)}) copy-start(s32[256]{0:T(256)} %param.31) | copy-start | bytes 3076
  22.0 12.8 %copy-start.8 = (f32[256,9]{1,0:T(8,128)S(1)}, f32[256,9]{1,0:T(8,128)}, u32[]{:S(2)}) copy-start(f32[256,9]{1,0:T(8,128)} %constant.105.clone) | copy-start | bytes 27652
  22.0 13.1 %copy-start.7 = (f32[256,9]{1,0:T(8,128)S(1)}, f32[256,9]{1,0:T(8,128)}, u32[]{:S(2)}) copy-start(f32[256,9]{1,0:T(8,128)} %constant.107.clone) | copy-start | bytes 27652
  22.0 13.3 %copy-start.6 = (f32[9,256]{1,0:T(8,128)S(1)}, f32[9,256]{1,0:T(8,128)}, u32[]{:S(2)}) copy-start(f32[9,256]{1,0:T(8,128)} %constant.106.clone) | copy-start | bytes 27652
  22.0 13.7 %copy-start.4 = (f32[256,256]{1,0:T(8,128)S(1)}, f32[256,256]{1,0:T(8,128)}, u32[]{:S(2)}) copy-start(f32[256,256]{1,0:T(8,128)} %constant.109.clone) | copy-start | bytes 786436
  22.0 13.7 %copy-start.5 = (f32[9,256]{1,0:T(8,128)S(1)}, f32[9,256]{1,0:T(8,128)}, u32[]{:S(2)}) copy-start(f32[9,256]{1,0:T(8,128)} %constant.108.clone) | copy-start | bytes 27652
  22.0 14.7 %copy-start.13 = (s32[128]{0:T(128)S(1)}, s32[128]{0:T(128)}, u32[]{:S(2)}) copy-start(s32[128]{0:T(128)} %get-tuple-element.8) | copy-start | bytes 1540
  22.0 15.0 %copy-start.9 = (bf16[4,4608]{1,0:T(4,128)(2,1)S(1)}, bf16[4,4608]{1,0:T(4,128)(2,1)}, u32[]{:S(2)}) copy-start(bf16[4,4608]{1,0:T(4,128)(2,1)} %constant.154) | copy-start | bytes 110596
  22.0 61.5 %all-to-all-start.1 = ((f32[32,8,16,128]{3,2,1,0:T(8,128)}), f32[32,8,16,128]{3,2,1,0:T(8,128)S(1)}, u32[]{:S(2)}, u32[]{:S(2)}) async-start(f32[32,8,16,128]{3,2,1,0:T(8,128)} %bitcast.65), calls=%async_computation.1 | async-start | bytes 4194304 | tf_op jit(solution)/shard_map/all_to_all | solution.py:433
  38.3 2.5 %copy-start.3 = (f32[512,256]{1,0:T(8,128)S(1)}, f32[512,256]{1,0:T(8,128)}, u32[]{:S(2)}) copy-start(f32[512,256]{1,0:T(8,128)} %constant.111.clone) | copy-start | bytes 1572868
  39.3 2.8 %copy-start.2 = (f32[512,256]{1,0:T(8,128)S(1)}, f32[512,256]{1,0:T(8,128)}, u32[]{:S(2)}) copy-start(f32[512,256]{1,0:T(8,128)} %constant.112.clone) | copy-start | bytes 1572868
  83.5 1.4 copy-start.1

commit v2 on v1

v2 whole, which is shorter than its diff:
```python
import functools

import jax
import jax.numpy as jnp
import numpy as np
from jax import lax
from jax.experimental import pallas as pl
from jax.experimental.pallas import tpu as pltpu
from jax.sharding import PartitionSpec as P

MESH_X = 16
PER_SIDE = 9
SPECIES = 3
NS = PER_SIDE * PER_SIDE * SPECIES
LANES = 256
COUPLING = 0.2
SWEEPS = 3
GROUPS = 4
F32 = jnp.float32
BF16 = jnp.bfloat16
HIGHEST = lax.Precision.HIGHEST
MESH = pl.DeviceIdType.MESH
SOUTH, EAST, NORTH, WEST = 0, 1, 2, 3
VMEM_LIMIT = 60 * 1024 * 1024

NN_DIMS = (((1,), (0,)), ((), ()))
NT_DIMS = (((1,), (1,)), ((), ()))
TN_DIMS = (((0,), (0,)), ((), ()))


def split(x):
    high = x.astype(BF16)
    return high, (x - high.astype(F32)).astype(BF16)


def dot(a, b, dims=NN_DIMS):
    return lax.dot_general(a, b, dims, preferred_element_type=F32)


def dot3(a, b, dims=NN_DIMS):
    return dot(a[0], b[0], dims) + dot(a[0], b[1], dims) + dot(a[1], b[0], dims)


def edge_lists():
    last = PER_SIDE - 1
    return [
        [i for i in range(PER_SIDE)],
        [i * PER_SIDE + last for i in range(PER_SIDE)],
        [last * PER_SIDE + last - i for i in range(PER_SIDE)],
        [(last - i) * PER_SIDE for i in range(PER_SIDE)],
    ]


def selection_tables():
    pair = np.zeros((2, LANES, 128), np.float32)
    pair_s = np.full((LANES,), -1)
    for lane in range(NS):
        node, s = divmod(lane, SPECIES)
        pair[0, lane, node // PER_SIDE] = 1.0
        pair[1, lane, node % PER_SIDE] = 1.0
        pair_s[lane] = s
    trace = np.zeros((4, 128, 128), np.float32)
    trace_s = np.full((128,), -2)
    for d, nodes in enumerate(edge_lists()):
        for t in range(PER_SIDE):
            for s in range(SPECIES):
                lane = d * 32 + t * SPECIES + s
                trace_s[lane] = s
                back = nodes[PER_SIDE - 1 - t]
                trace[0, lane, nodes[t] // PER_SIDE] = 1.0
                trace[1, lane, nodes[t] % PER_SIDE] = 1.0
                trace[2, lane, back // PER_SIDE] = 1.0
                trace[3, lane, back % PER_SIDE] = 1.0
    pair_mask = (pair_s[:, None] == pair_s[None, :]) & (pair_s[:, None] >= 0)
    trace_mask = trace_s[:, None] == pair_s[None, :]
    hot = np.concatenate([pair.reshape(2 * LANES, 128), trace.reshape(512, 128)], axis=0)
    mask = np.concatenate([pair_mask, trace_mask], axis=0)
    return jnp.asarray(hot.astype(BF16)), jnp.asarray(mask.astype(np.float32))


def transform_tables(planes):
    modes = planes // 2
    phase = (np.arange(modes)[:, None] * np.arange(planes)[None, :]) % planes
    angle = phase.astype(np.float64) * (2.0 * np.pi / planes)
    trig = np.concatenate([np.cos(angle), -np.sin(angle)], axis=0)
    weight = np.where(np.arange(modes) == 0, 1.0, 2.0)
    weight = np.concatenate([weight, weight])
    return np.float32(trig / planes), np.float32((trig * weight[:, None]).T)


def split_table(table):
    high = table.astype(BF16)
    low = (table - high.astype(np.float32)).astype(BF16)
    return jnp.asarray(np.stack([high, low]))


def split3(x):
    high = x.astype(BF16)
    rest = x - high.astype(F32)
    middle = rest.astype(BF16)
    return high, middle, (rest - middle.astype(F32)).astype(BF16)


def pick(hot, x, dims=NN_DIMS):
    return sum(dot(hot, part, dims) for part in split3(x))


def pick_right(x, hot):
    return sum(dot(part, hot, NT_DIMS) for part in split3(x))


def finish_kernel(n_span, depth, own, values_ref, place_ref, out_ref):
    place = place_ref[...].astype(BF16)
    for plane in range(depth):
        for h in range(2):
            parts = [
                values_ref[pl.ds((h * 4 + e) * depth + plane, n_span, stride=8 * depth), :]
                for e in range(4)
            ]
            high, low = split(jnp.concatenate(parts, axis=0))
            moved = dot(high, place, TN_DIMS) + dot(low, place, TN_DIMS)
            count = min(NS - h * 128, 128)
            out_ref[pl.ds(h * 128 * depth + plane, count, stride=depth), :] = moved[:count]


def neighbours(n_span, n_elem, block_rows):
    span, elem = lax.axis_index("span"), lax.axis_index("elem")
    x = span % block_rows
    odd = elem % 2
    up = 1 - 2 * odd
    block_row = jnp.where(odd == 1, block_rows - 1 - x, x)
    last, first = block_row == block_rows - 1, block_row == 0
    return {
        NORTH: (jnp.where(last, span, span + up), jnp.where(last, (elem + 1) % n_elem, elem)),
        SOUTH: (jnp.where(first, span, span - up), jnp.where(first, (elem + n_elem - 1) % n_elem, elem)),
        EAST: ((span + block_rows) % n_span, elem),
        WEST: ((span + n_span - block_rows) % n_span, elem),
    }


def main_kernel(
    n_span,
    n_elem,
    depth,
    own,
    cols,
    species_hbm,
    laplacian_hbm,
    binary_ref,
    dref_ref,
    eig_ref,
    basis_ref,
    rounds_ref,
    adjacency_ref,
    edge_map_ref,
    hot_ref,
    mask_ref,
    forward_hbm,
    backward_hbm,
    result_ref,
    place_ref,
    species_ref,
    laplacian_ref,
    source_ref,
    tables_ref,
    walk_ref,
    turn_ref,
    small_ref,
    forward_ref,
    backward_ref,
    sent_ref,
    values_ref,
    back_ref,
    work_high,
    work_low,
    rhs_ref,
    modal_ref,
    inverse_ref,
    rounds_col,
    trace_ref,
    send_ref,
    recv_ref,
    load_sem,
    walk_sem,
    table_send,
    table_recv,
    out_send,
    out_recv,
    back_send,
    back_recv,
    send_sem,
    recv_sem,
):
    planes = n_span * depth
    modes = planes // 2
    rows = own // cols
    block_rows = rows // 2
    group = planes // GROUPS
    half = group // 2
    tile = min(256, planes)
    block = 8 * depth
    nodes = PER_SIDE * PER_SIDE
    span, elem = lax.axis_index("span"), lax.axis_index("elem")
    near = neighbours(n_span, n_elem, block_rows)

    def span_peer(k):
        z = (span // block_rows + k // block_rows) % (n_span // block_rows)
        x = (span + k) % block_rows
        return z * block_rows + x

    barrier = pltpu.get_barrier_semaphore()

    def greet_span(k, carry):
        pl.semaphore_signal(barrier, inc=1, device_id=(span_peer(k), elem), device_id_type=MESH)
        return carry

    def greet_elem(k, carry):
        pl.semaphore_signal(
            barrier, inc=1, device_id=(span, (elem + k) % n_elem), device_id_type=MESH
        )
        return carry

    lax.fori_loop(1, n_elem, greet_elem, 0)
    lax.fori_loop(1, n_span, greet_span, 0)

    cut = (128 + SPECIES - 1) // SPECIES
    pieces = [(0, cut), (cut, nodes - cut)]
    loads = []
    for i, (first, count) in enumerate(pieces):
        span_rows = pl.ds(first * SPECIES * depth, count * SPECIES * depth)
        for j, (source, target) in enumerate(
            ((species_hbm, species_ref), (laplacian_hbm, laplacian_ref))
        ):
            copy = pltpu.make_async_copy(source.at[span_rows], target.at[span_rows], load_sem.at[i * 2 + j])
            copy.start()
            loads.append(copy)
    table_loads = [
        pltpu.make_async_copy(forward_hbm, forward_ref, load_sem.at[4]),
        pltpu.make_async_copy(backward_hbm, backward_ref, load_sem.at[5]),
    ]
    for copy in table_loads:
        copy.start()

    inverse = [[1.0 / binary_ref[s, j] for j in range(SPECIES + 1)] for s in range(SPECIES)]
    dref = [dref_ref[s] for s in range(SPECIES)]
    over = [1.0 / dref_ref[s] for s in range(SPECIES)]

    def sources(first, count):
        def one_node(node, carry):
            base = pl.multiple_of(node * SPECIES * depth, 8)
            parts = [species_ref[pl.ds(base + s * depth, depth), :] for s in range(SPECIES)]
            slopes = [laplacian_ref[pl.ds(base + s * depth, depth), :] for s in range(SPECIES)]
            bath = 1.0 - (parts[0] + parts[1] + parts[2])
            for s in range(SPECIES):
                resistance = bath * inverse[s][SPECIES]
                for j in range(SPECIES):
                    if j != s:
                        resistance = resistance + parts[j] * inverse[s][j]
                mixture = (1.0 - parts[s]) / resistance
                value = (parts[s] + (mixture - dref[s]) * slopes[s]) * over[s]
                source_ref[pl.ds(base + s * depth, depth), :] = value
            return carry

        lax.fori_loop(first, first + count, one_node, 0, unroll=2)

    source_ref[pl.ds(NS * depth, (LANES - NS) * depth), :] = jnp.zeros(((LANES - NS) * depth, own), F32)
    loads[0].wait()
    loads[1].wait()
    sources(*pieces[0])

    ahead_id, ahead_edge = adjacency_ref[...], edge_map_ref[...]
    owner = ahead_id // own
    step = owner * (8 * own) + (ahead_edge + 2) % 4 * own + ahead_id % own
    before = (elem + n_elem - 1) % n_elem
    edge_ids = lax.broadcasted_iota(jnp.int32, (4, own), 0)
    elem_ids = lax.broadcasted_iota(jnp.int32, (4, own), 1)
    facing = jnp.where(owner == before, (edge_ids + 2) % 4 * own + elem_ids, 8 * own)
    start = jnp.min(jnp.min(facing, axis=0, keepdims=True), axis=1, keepdims=True)
    my_rows = pl.ds(pl.multiple_of(elem * 8, 8), 8)
    tables_ref[my_rows, :] = jnp.concatenate([step, jnp.broadcast_to(start, (4, own))], axis=0)

    pl.semaphore_wait(barrier, n_span + n_elem - 2)

    def table_copy(k):
        return pltpu.make_async_remote_copy(
            src_ref=tables_ref.at[my_rows],
            dst_ref=tables_ref.at[my_rows],
            send_sem=table_send.at[k],
            recv_sem=table_recv.at[k],
            device_id=(span, (elem + k) % n_elem),
            device_id_type=MESH,
        )

    for k in range(1, n_elem):
        table_copy(k).start()
    loads[2].wait()
    loads[3].wait()
    sources(*pieces[1])
    for k in range(1, n_elem):
        table_copy(k).wait_recv()
    walk = pltpu.make_async_copy(tables_ref, walk_ref, walk_sem)
    walk.start()
    walk.wait()

    def ahead(dart):
        return walk_ref[dart // own, dart % own]

    odd = elem % 2
    dart = lax.fori_loop(0, rows * elem, lambda i, d: ahead(d), walk_ref[4, 0])
    norths = []
    for row in range(rows):
        norths.append(dart)
        if row + 1 < rows:
            dart = ahead(dart)
    easts = []
    for dart in norths:
        edge = dart // own % 8
        easts.append(dart + ((edge + 3) % 4 - edge) * own)
    lane = lax.broadcasted_iota(jnp.int32, (1, own), 1)
    for col in range(cols):
        for row in range(rows):
            dart = easts[row]
            block_row = row // 2
            x = jnp.where(odd == 1, block_rows - 1 - block_row, block_row)
            slot = (row % 2 * 2 + col % 2) * n_span + (col // 2) * block_rows + x
            turn_ref[slot] = (dart // own % 8 + 3) % 4
            place_ref[pl.ds(slot, 1), :] = (lane == dart % own).astype(F32)
            if col + 1 < cols:
                easts[row] = ahead(dart)

    def exchange(source, target, send, recv, k, h):
        peer = span_peer(k)
        return pltpu.make_async_remote_copy(
            src_ref=source.at[pl.ds(pl.multiple_of(peer * block + h * (block // 2), 8), block // 2)],
            dst_ref=target.at[pl.ds(pl.multiple_of(span * block + h * (block // 2), 8), block // 2)],
            send_sem=send.at[h, k],
            recv_sem=recv.at[h, k],
            device_id=(peer, elem),
            device_id_type=MESH,
        )

    def send_phase(source, target, send, recv, h):
        def one(k, carry):
            exchange(source, target, send, recv, k, h).start()
            return carry

        lax.fori_loop(1, n_span, one, 0)
        mine = pl.ds(pl.multiple_of(span * block + h * (block // 2), 8), block // 2)
        target[mine, :] = source[mine, :]

    def wait_phase(source, target, send, recv, h, sending):
        def one(k, carry):
            copy = exchange(source, target, send, recv, k, h)
            if sending:
                copy.wait_send()
            else:
                copy.wait_recv()
            return carry

        lax.fori_loop(1, n_span, one, 0)

    place = place_ref[...].astype(BF16)
    for h in range(2):
        for plane in range(depth):
            high, low = split(source_ref[pl.ds(h * 128 * depth + plane, 128, stride=depth), :])
            moved = dot(place, high, NT_DIMS) + dot(place, low, NT_DIMS)
            for e in range(4):
                sent_ref[pl.ds((h * 4 + e) * depth + plane, n_span, stride=block), :] = moved[
                    e * n_span : (e + 1) * n_span
                ]
        send_phase(sent_ref, values_ref, out_send, out_recv, h)

    small_ref[...] = jnp.zeros_like(small_ref)
    small_ref[:PER_SIDE, :PER_SIDE] = basis_ref[...]
    small_ref[128 : 128 + 1, :PER_SIDE] = eig_ref[...]
    basis = small_ref[:128, :]
    hot_i, hot_j = hot_ref[:LANES, :], hot_ref[LANES : 2 * LANES, :]

    def spread(left_i, left_j):
        return pick_right(pick(left_i, basis), hot_i) * pick_right(pick(left_j, basis), hot_j)

    traces_hot = [hot_ref[pl.ds(2 * LANES + i * 128, 128), :] for i in range(4)]
    trace_mask = mask_ref[LANES:, :]
    pair = split(spread(hot_i, hot_j) * mask_ref[:LANES, :])
    out_trace = spread(traces_hot[0], traces_hot[1]) * trace_mask
    in_trace = spread(traces_hot[2], traces_hot[3]) * (COUPLING * trace_mask)

    def turned(matrix, e):
        turn = jnp.full((32, LANES), turn_ref[e * n_span + span], jnp.int32)
        edges = [matrix[d * 32 : (d + 1) * 32] for d in range(4)]
        blocks = []
        for d in range(4):
            chosen = edges[d]
            for r in range(1, 4):
                chosen = jnp.where(turn == r, edges[(d + r) % 4], chosen)
            blocks.append(chosen)
        return split(jnp.concatenate(blocks, axis=0))

    to_trace = [turned(out_trace, e) for e in range(4)]
    from_trace = [turned(in_trace, e) for e in range(4)]

    eig_row = small_ref[128:136, :]
    diag = (pick_right(eig_row, hot_i) + pick_right(eig_row, hot_j))[:1]
    pair_lane = lax.broadcasted_iota(jnp.int32, (1, LANES), 1)
    for s in range(SPECIES):
        diag = diag + jnp.where(pair_lane % SPECIES == s, over[s], 0.0)
    row = lax.broadcasted_iota(jnp.int32, (planes, LANES), 0)
    wave = jnp.where(row >= modes, row - modes, row).astype(F32) * (8.0 / planes)
    inverse_ref[...] = 1.0 / (wave * wave + diag)
    square = lax.broadcasted_iota(jnp.int32, (modes, modes), 0) == lax.broadcasted_iota(
        jnp.int32, (modes, modes), 1
    )
    spread_rounds = jnp.where(square, rounds_ref[...].astype(F32), 0.0).astype(BF16)
    column = dot(spread_rounds, jnp.ones((modes, 128), BF16))
    rounds_col[:modes, :] = column
    rounds_col[modes:, :] = column

    table_loads[0].wait()
    for h in range(2):
        wait_phase(sent_ref, values_ref, out_send, out_recv, h, False)
        for e in (0, 2):
            lanes = []
            for i in range(2):
                first = (h * 4 + e + i) * depth
                lanes.append(
                    jnp.concatenate(
                        [values_ref[pl.ds(d * block + first, depth), :] for d in range(n_span)], axis=0
                    )
                )
            planes_in = split(jnp.concatenate(lanes, axis=1))
            for first in range(0, planes, tile):
                out_rows = pl.ds(first, tile)
                value = split(dot3((forward_ref[0, out_rows, :], forward_ref[1, out_rows, :]), planes_in))
                for i in range(2):
                    target = pl.ds((e + i) * LANES + h * 128, 128)
                    work_high[out_rows, target] = value[0][:, i * 128 : (i + 1) * 128]
                    work_low[out_rows, target] = value[1][:, i * 128 : (i + 1) * 128]

    lane_group = lax.broadcasted_iota(jnp.int32, (1, 128), 1) // 32
    outer = {NORTH: (2, 3), SOUTH: (0, 1), EAST: (1, 3), WEST: (0, 2)}
    opposite = {NORTH: SOUTH, SOUTH: NORTH, EAST: WEST, WEST: EAST}

    def copies(sweep, g):
        return [
            pltpu.make_async_remote_copy(
                src_ref=send_ref.at[sweep, g, d],
                dst_ref=recv_ref.at[sweep, g, opposite[d]],
                send_sem=send_sem.at[sweep, g, d],
                recv_sem=recv_sem.at[sweep, g, opposite[d]],
                device_id=near[d],
                device_id_type=MESH,
            )
            for d in range(4)
        ]

    def send_traces(sweep, g):
        g_rows = pl.ds(g * group, group)
        traces = []
        for e in range(4):
            trace = dot3(split(modal_ref[e, g_rows, :]), to_trace[e], NT_DIMS)
            trace_ref[e, g_rows, :] = trace
            traces.append(trace)
        for d in range(4):
            packed = None
            for h in range(2):
                for q in range(2):
                    piece = traces[outer[d][q]][h * half : (h + 1) * half]
                    goal = h * 2 + q
                    shift = (goal - d) % 4 * 32
                    if shift:
                        piece = pltpu.roll(piece, shift, 1)
                    packed = piece if packed is None else jnp.where(lane_group == goal, piece, packed)
            send_ref[sweep, g, d] = packed
        for copy in copies(sweep, g):
            copy.start()

    def update(sweep, g):
        for copy in copies(sweep, g):
            copy.wait_recv()
        for h in range(2):
            h_rows = pl.ds(g * group + h * half, half)
            active = rounds_col[h_rows, :] > sweep + 1.5
            active = jnp.concatenate([active, active], axis=1)
            scale = inverse_ref[h_rows, :]
            for e in range(4):
                a, b = divmod(e, 2)
                across = None
                sides = (
                    (NORTH, None) if a == 0 else (NORTH, b),
                    (SOUTH, b) if a == 0 else (SOUTH, None),
                    (EAST, None) if b == 0 else (EAST, a),
                    (WEST, a) if b == 0 else (WEST, None),
                )
                for d, q in sides:
                    if q is None:
                        other = (2 * (1 - a) + b) if d in (NORTH, SOUTH) else (2 * a + 1 - b)
                        piece = pltpu.roll(trace_ref[other, h_rows, :], 64, 1)
                    else:
                        piece = recv_ref[sweep, g, d]
                        shift = (d - (h * 2 + q)) % 4 * 32
                        if shift:
                            piece = pltpu.roll(piece, shift, 1)
                    across = piece if across is None else jnp.where(lane_group == d, piece, across)
                fresh = (rhs_ref[e, h_rows, :] + dot3(split(across), from_trace[e])) * scale
                modal_ref[e, h_rows, :] = jnp.where(active, fresh, modal_ref[e, h_rows, :])

    for g in range(GROUPS):
        g_rows = pl.ds(g * group, group)
        scale = inverse_ref[g_rows, :]
        for e in range(4):
            lanes = pl.ds(e * LANES, LANES)
            rhs = dot3((work_high[g_rows, lanes], work_low[g_rows, lanes]), pair)
            rhs_ref[e, g_rows, :] = rhs
            modal_ref[e, g_rows, :] = rhs * scale
        send_traces(0, g)
    for sweep in range(SWEEPS):
        for g in range(GROUPS):
            update(sweep, g)
            if sweep + 1 < SWEEPS:
                send_traces(sweep + 1, g)

    for e in range(4):
        for first in range(0, planes, tile):
            out_rows = pl.ds(first, tile)
            high, low = split(dot3(split(modal_ref[e, out_rows, :]), pair, NT_DIMS))
            work_high[out_rows, pl.ds(e * LANES, LANES)] = high
            work_low[out_rows, pl.ds(e * LANES, LANES)] = low
    table_loads[1].wait()
    for h in range(2):
        for e in (0, 2):
            lanes = [pl.ds((e + i) * LANES + h * 128, 128) for i in range(2)]
            coeffs = tuple(
                jnp.concatenate([ref[:, lanes[0]], ref[:, lanes[1]]], axis=1) for ref in (work_high, work_low)
            )
            for first in range(0, planes, tile):
                out_rows = pl.ds(first, tile)
                value = dot3((backward_ref[0, out_rows, :], backward_ref[1, out_rows, :]), coeffs)
                for i in range(2):
                    for d in range(tile // depth):
                        goal = (first // depth + d) * block + (h * 4 + e + i) * depth
                        back_ref[pl.ds(goal, depth), :] = value[
                            d * depth : (d + 1) * depth, i * 128 : (i + 1) * 128
                        ]
        send_phase(back_ref, result_ref, back_send, back_recv, h)
    for k in range(1, n_elem):
        table_copy(k).wait_send()
    for h in range(2):
        wait_phase(sent_ref, values_ref, out_send, out_recv, h, True)
    for sweep in range(SWEEPS):
        for g in range(GROUPS):
            for copy in copies(sweep, g):
                copy.wait_send()
    for h in range(2):
        wait_phase(back_ref, result_ref, back_send, back_recv, h, True)
        wait_phase(back_ref, result_ref, back_send, back_recv, h, False)


def vmem():
    return pl.BlockSpec(memory_space=pltpu.VMEM)


def smem():
    return pl.BlockSpec(memory_space=pltpu.SMEM)


def hbm():
    return pl.BlockSpec(memory_space=pl.ANY)


def body(species, laplacian, binary, dref, stiff_eig, basis, rounds, adjacency, edge_map):
    n_span = lax.axis_size("span")
    n_elem = lax.axis_size("elem")
    depth = species.shape[2]
    own = species.shape[3]
    planes = depth * n_span
    flat = n_span * 8 * depth
    forward, backward = transform_tables(planes)
    hot, mask = selection_tables()
    halo = (SWEEPS, GROUPS, 4, planes // GROUPS // 2, 128)
    dma = pltpu.SemaphoreType.DMA
    returned, place = pl.pallas_call(
        functools.partial(main_kernel, n_span, n_elem, depth, own, MESH_X),
        out_shape=(
            jax.ShapeDtypeStruct((flat, 128), F32),
            jax.ShapeDtypeStruct((own, own), F32),
        ),
        in_specs=[hbm(), hbm(), smem(), smem()] + [vmem()] * 7 + [hbm(), hbm()],
        out_specs=(vmem(), vmem()),
        scratch_shapes=[
            pltpu.VMEM((NS * depth, own), F32),
            pltpu.VMEM((NS * depth, own), F32),
            pltpu.VMEM((LANES * depth, own), F32),
            pltpu.VMEM((n_elem * 8, own), jnp.int32),
            pltpu.SMEM((n_elem * 8, own), jnp.int32),
            pltpu.SMEM((own,), jnp.int32),
            pltpu.VMEM((136, 128), F32),
            pltpu.VMEM((2, planes, planes), BF16),
            pltpu.VMEM((2, planes, planes), BF16),
            pltpu.VMEM((flat, 128), F32),
            pltpu.VMEM((flat, 128), F32),
            pltpu.VMEM((flat, 128), F32),
            pltpu.VMEM((planes, 4 * LANES), BF16),
            pltpu.VMEM((planes, 4 * LANES), BF16),
            pltpu.VMEM((4, planes, LANES), F32),
            pltpu.VMEM((4, planes, LANES), F32),
            pltpu.VMEM((planes, LANES), F32),
            pltpu.VMEM((planes, 128), F32),
            pltpu.VMEM((4, planes, 128), F32),
            pltpu.VMEM(halo, F32),
            pltpu.VMEM(halo, F32),
            dma((6,)),
            dma,
            dma((n_elem,)),
            dma((n_elem,)),
            dma((2, n_span)),
            dma((2, n_span)),
            dma((2, n_span)),
            dma((2, n_span)),
            dma(halo[:3]),
            dma(halo[:3]),
        ],
        compiler_params=pltpu.CompilerParams(
            collective_id=0, has_side_effects=True, vmem_limit_bytes=VMEM_LIMIT
        ),
        name="main",
    )(
        species.reshape(NS * depth, own),
        laplacian.reshape(NS * depth, own),
        binary,
        dref,
        stiff_eig.reshape(1, PER_SIDE),
        basis,
        rounds.reshape(1, planes // 2),
        adjacency.T,
        edge_map.T,
        hot,
        mask,
        split_table(forward),
        split_table(backward),
    )
    updated = pl.pallas_call(
        functools.partial(finish_kernel, n_span, depth, own),
        out_shape=jax.ShapeDtypeStruct((NS * depth, own), F32),
        in_specs=[vmem(), vmem()],
        out_specs=vmem(),
        compiler_params=pltpu.CompilerParams(vmem_limit_bytes=VMEM_LIMIT),
        name="finish",
    )(returned, place)
    return updated.reshape(species.shape)


def solution(mesh):
    return jax.shard_map(
        body,
        mesh=mesh,
        in_specs=(
            P(None, None, "span", "elem"),
            P(None, None, "span", "elem"),
            P(),
            P(),
            P(),
            P(),
            P(),
            P("elem", None),
            P("elem", None),
        ),
        out_specs=P(None, None, "span", "elem"),
        check_vma=False,
    )
```

time: 174 us -> 145 us (0.83)
  Pallas kernels: 42.7 us -> 145 us
  blocking collectives: 65.3 us -> 0 us
  waiting for transfers between devices: 40 us -> 0 us
  starting transfers between devices: 11.7 us -> 0 us
  matrix products: 7.27 us -> 0 us
  local copies, waits for them, and re-layouts: 4.25 us -> 0 us
    pallas_call x3 -> x1, Pallas kernels: 37.5 us -> 140 us  [body(): pl.pallas_call(functools.partial(main_kernel, n_span, n_elem, depth, own,...]
    all_to_all x2 -> x0, blocking collectives: 65.3 us -> none  [the longest x1 55.5 us: body(): lax.all_to_all(solved, 'span', split_axis=0, concat_axis=0, tiled=True)]
    all_to_all x1 -> x0, waiting for transfers between devices: 40 us -> none  [body(): lax.all_to_all(sent.reshape(n_span, 8, depth, 128), 'span', split_axis=0,...]
    all_to_all x1 -> x0, starting transfers between devices: 11.7 us -> none  [body(): lax.all_to_all(sent.reshape(n_span, 8, depth, 128), 'span', split_axis=0,...]
    dot_general x13 -> x0, matrix products: 7.27 us -> none  [the longest x3 3.78 us: spread(): jnp.dot(jnp.dot(left_j, matrix, precision=HIGHEST), right_j.T, precision=...]
  transfers between devices with their start and end apart: 1 -> 0, of which waited for: 1 -> 0; matrix products, arithmetic and copies ran while one was open for 6% -> 0% of each run, Pallas kernels for 0% -> 0%
where the time goes in v2:
time: 145 us
  Pallas kernels  145 us (100%)
    pallas_call x1, Pallas kernels, body(): pl.pallas_call(functools.partial(main_kernel, n_span, n_elem, depth, own,...  140 us
    pallas_call x1, Pallas kernels, body(): pl.pallas_call(functools.partial(finish_kernel, n_span, depth, own), out_...  5.49 us

profile of v2, /device:TPU:6, one launch (start us, length us, event | category | flops | bytes accessed | tf_op | source)
XLA Modules:
  0.0 145.2 jit_solution(17541941415854262909)
XLA Ops:
  0.0 139.7 %main.1 = (f32[4096,128]{1,0:T(8,128)}, f32[128,128]{1,0:T(8,128)}) custom-call(f32[3888,128]{1,0:T(8,128)} %bitcast.7, f32[3888,128]{1,0:T(8,128)} %bitcast.8, f32[3,4]{1,0:T(4,128)} %binary_ref.1, f32[3]{0:T(128)} %dref_ref.1, f32[1,9]{1,0:T(1,128)} %bitcast.12, f32[9,9]{1,0:T(8,128)} %basis_ref.1, s32[1,256]{1,0:T(1,128)} %bitcast.11, s32[4,128]{1,0:T(4,128)} %bitcast.9, ...), custom_call_target="tpu_custom_call" | custom-call | tf_op jit(solution)/shard_map/main/pallas_call | solution.py:581
  139.7 5.5 %finish.1 = f32[3888,128]{1,0:T(8,128)} custom-call(f32[4096,128]{1,0:T(8,128)} %get-tuple-element.7.values_ref, f32[128,128]{1,0:T(8,128)} %get-tuple-element.8.place_ref), custom_call_target="tpu_custom_call" | custom-call | tf_op jit(solution)/shard_map/finish/pallas_call | solution.py:641

commit v3 on v2

--- a/solution.py
+++ b/solution.py
@@ -109,18 +109,44 @@
     return sum(dot(part, hot, NT_DIMS) for part in split3(x))
 
 
-def finish_kernel(n_span, depth, own, values_ref, place_ref, out_ref):
+def place_back(n_span, depth, h, values_ref, stride, place, out_ref):
+    count = min(NS - h * 128, 128)
+    for first in range(0, depth, 8):
+        parts = [
+            values_ref[pl.ds(d * stride + e * depth + first, 8), :] for e in range(4) for d in range(n_span)
+        ]
+        by_plane = jnp.transpose(jnp.stack(parts, axis=0), (1, 0, 2))
+        moved = []
+        for plane in range(8):
+            high, low = split(by_plane[plane])
+            moved.append(dot(high, place, TN_DIMS) + dot(low, place, TN_DIMS))
+        by_lane = jnp.transpose(jnp.stack(moved, axis=0), (1, 0, 2))
+        for lane in range(count):
+            out_ref[pl.ds(lane * depth + first, 8), :] = by_lane[lane]
+
+
+def finish_kernel(
+    n_span, depth, own, half_hbm, values_hbm, place_ref, out_hbm, half_ref, values_ref, tail_ref, sems
+):
+    loads = [
+        pltpu.make_async_copy(values_hbm, values_ref, sems.at[0]),
+        pltpu.make_async_copy(half_hbm, half_ref, sems.at[1]),
+    ]
+    for copy in loads:
+        copy.start()
+    split_row = 128 * depth
+    stores = [
+        pltpu.make_async_copy(half_ref, out_hbm.at[pl.ds(0, split_row)], sems.at[2]),
+        pltpu.make_async_copy(tail_ref, out_hbm.at[pl.ds(split_row, NS * depth - split_row)], sems.at[3]),
+    ]
+    loads[1].wait()
+    stores[0].start()
     place = place_ref[...].astype(BF16)
-    for plane in range(depth):
-        for h in range(2):
-            parts = [
-                values_ref[pl.ds((h * 4 + e) * depth + plane, n_span, stride=8 * depth), :]
-                for e in range(4)
-            ]
-            high, low = split(jnp.concatenate(parts, axis=0))
-            moved = dot(high, place, TN_DIMS) + dot(low, place, TN_DIMS)
-            count = min(NS - h * 128, 128)
-            out_ref[pl.ds(h * 128 * depth + plane, count, stride=depth), :] = moved[:count]
+    loads[0].wait()
+    place_back(n_span, depth, 1, values_ref, 4 * depth, place, tail_ref)
+    stores[1].start()
+    stores[0].wait()
+    stores[1].wait()
 
 
 def neighbours(n_span, n_elem, block_rows):
@@ -138,6 +164,43 @@
     }
 
 
+def table_kernel(n_elem, own, adjacency_ref, edge_map_ref, tables_ref, table_send, table_recv):
+    span, elem = lax.axis_index("span"), lax.axis_index("elem")
+    barrier = pltpu.get_barrier_semaphore()
+    for k in range(1, n_elem):
+        pl.semaphore_signal(
+            barrier, inc=1, device_id=(span, (elem + k) % n_elem), device_id_type=MESH
+        )
+
+    ahead_id, ahead_edge = adjacency_ref[...], edge_map_ref[...]
+    owner = ahead_id // own
+    step = owner * (8 * own) + (ahead_edge + 2) % 4 * own + ahead_id % own
+    before = (elem + n_elem - 1) % n_elem
+    edge_ids = lax.broadcasted_iota(jnp.int32, (4, own), 0)
+    elem_ids = lax.broadcasted_iota(jnp.int32, (4, own), 1)
+    facing = jnp.where(owner == before, (edge_ids + 2) % 4 * own + elem_ids, 8 * own)
+    start = jnp.min(jnp.min(facing, axis=0, keepdims=True), axis=1, keepdims=True)
+    my_rows = pl.ds(pl.multiple_of(elem * 8, 8), 8)
+    tables_ref[my_rows, :] = jnp.concatenate([step, jnp.broadcast_to(start, (4, own))], axis=0)
+
+    pl.semaphore_wait(barrier, n_elem - 1)
+
+    def table_copy(k):
+        return pltpu.make_async_remote_copy(
+            src_ref=tables_ref.at[my_rows],
+            dst_ref=tables_ref.at[my_rows],
+            send_sem=table_send.at[k],
+            recv_sem=table_recv.at[k],
+            device_id=(span, (elem + k) % n_elem),
+            device_id_type=MESH,
+        )
+
+    for k in range(1, n_elem):
+        table_copy(k).start()
+    for k in range(1, n_elem):
+        table_copy(k).wait()
+
+
 def main_kernel(
     n_span,
     n_elem,
@@ -151,19 +214,17 @@
     eig_ref,
     basis_ref,
     rounds_ref,
-    adjacency_ref,
-    edge_map_ref,
+    walk_ref,
     hot_ref,
     mask_ref,
     forward_hbm,
     backward_hbm,
-    result_ref,
+    half_ref,
+    second_ref,
     place_ref,
     species_ref,
     laplacian_ref,
     source_ref,
-    tables_ref,
-    walk_ref,
     turn_ref,
     small_ref,
     forward_ref,
@@ -171,6 +232,7 @@
     sent_ref,
     values_ref,
     back_ref,
+    result_ref,
     work_high,
     work_low,
     rhs_ref,
@@ -181,9 +243,6 @@
     send_ref,
     recv_ref,
     load_sem,
-    walk_sem,
-    table_send,
-    table_recv,
     out_send,
     out_recv,
     back_send,
@@ -268,45 +327,17 @@
     loads[1].wait()
     sources(*pieces[0])
 
-    ahead_id, ahead_edge = adjacency_ref[...], edge_map_ref[...]
-    owner = ahead_id // own
-    step = owner * (8 * own) + (ahead_edge + 2) % 4 * own + ahead_id % own
-    before = (elem + n_elem - 1) % n_elem
-    edge_ids = lax.broadcasted_iota(jnp.int32, (4, own), 0)
-    elem_ids = lax.broadcasted_iota(jnp.int32, (4, own), 1)
-    facing = jnp.where(owner == before, (edge_ids + 2) % 4 * own + elem_ids, 8 * own)
-    start = jnp.min(jnp.min(facing, axis=0, keepdims=True), axis=1, keepdims=True)
-    my_rows = pl.ds(pl.multiple_of(elem * 8, 8), 8)
-    tables_ref[my_rows, :] = jnp.concatenate([step, jnp.broadcast_to(start, (4, own))], axis=0)
-
-    pl.semaphore_wait(barrier, n_span + n_elem - 2)
-
-    def table_copy(k):
-        return pltpu.make_async_remote_copy(
-            src_ref=tables_ref.at[my_rows],
-            dst_ref=tables_ref.at[my_rows],
-            send_sem=table_send.at[k],
-            recv_sem=table_recv.at[k],
-            device_id=(span, (elem + k) % n_elem),
-            device_id_type=MESH,
-        )
-
-    for k in range(1, n_elem):
-        table_copy(k).start()
     loads[2].wait()
     loads[3].wait()
     sources(*pieces[1])
-    for k in range(1, n_elem):
-        table_copy(k).wait_recv()
-    walk = pltpu.make_async_copy(tables_ref, walk_ref, walk_sem)
-    walk.start()
-    walk.wait()
+
+    shift = own.bit_length() - 1
 
     def ahead(dart):
-        return walk_ref[dart // own, dart % own]
+        return walk_ref[dart]
 
     odd = elem % 2
-    dart = lax.fori_loop(0, rows * elem, lambda i, d: ahead(d), walk_ref[4, 0])
+    dart = lax.fori_loop(0, rows * elem, lambda i, d: ahead(d), walk_ref[4 * own])
     norths = []
     for row in range(rows):
         norths.append(dart)
@@ -314,25 +345,29 @@
             dart = ahead(dart)
     easts = []
     for dart in norths:
-        edge = dart // own % 8
-        easts.append(dart + ((edge + 3) % 4 - edge) * own)
+        edge = (dart >> shift) & 7
+        easts.append(dart + ((((edge + 3) & 3) - edge) << shift))
     lane = lax.broadcasted_iota(jnp.int32, (1, own), 1)
+    places = [jnp.where(odd == 1, block_rows - 1 - i, i) for i in range(block_rows)]
     for col in range(cols):
         for row in range(rows):
             dart = easts[row]
-            block_row = row // 2
-            x = jnp.where(odd == 1, block_rows - 1 - block_row, block_row)
-            slot = (row % 2 * 2 + col % 2) * n_span + (col // 2) * block_rows + x
-            turn_ref[slot] = (dart // own % 8 + 3) % 4
-            place_ref[pl.ds(slot, 1), :] = (lane == dart % own).astype(F32)
+            slot = (row % 2 * 2 + col % 2) * n_span + (col // 2) * block_rows + places[row // 2]
+            turn_ref[slot] = dart
+            place_ref[pl.ds(slot, 1), :] = (lane == (dart & (own - 1))).astype(F32)
             if col + 1 < cols:
                 easts[row] = ahead(dart)
+
+    def landing(target, h):
+        if isinstance(target, tuple):
+            return target[h].at[pl.ds(pl.multiple_of(span * (block // 2), 8), block // 2)]
+        return target.at[pl.ds(pl.multiple_of(span * block + h * (block // 2), 8), block // 2)]
 
     def exchange(source, target, send, recv, k, h):
         peer = span_peer(k)
         return pltpu.make_async_remote_copy(
             src_ref=source.at[pl.ds(pl.multiple_of(peer * block + h * (block // 2), 8), block // 2)],
-            dst_ref=target.at[pl.ds(pl.multiple_of(span * block + h * (block // 2), 8), block // 2)],
+            dst_ref=landing(target, h),
             send_sem=send.at[h, k],
             recv_sem=recv.at[h, k],
             device_id=(peer, elem),
@@ -346,7 +381,7 @@
 
         lax.fori_loop(1, n_span, one, 0)
         mine = pl.ds(pl.multiple_of(span * block + h * (block // 2), 8), block // 2)
-        target[mine, :] = source[mine, :]
+        landing(target, h)[...] = source[mine, :]
 
     def wait_phase(source, target, send, recv, h, sending):
         def one(k, carry):
@@ -359,15 +394,18 @@
 
         lax.fori_loop(1, n_span, one, 0)
 
+    pl.semaphore_wait(barrier, n_span + n_elem - 2)
     place = place_ref[...].astype(BF16)
     for h in range(2):
-        for plane in range(depth):
-            high, low = split(source_ref[pl.ds(h * 128 * depth + plane, 128, stride=depth), :])
-            moved = dot(place, high, NT_DIMS) + dot(place, low, NT_DIMS)
-            for e in range(4):
-                sent_ref[pl.ds((h * 4 + e) * depth + plane, n_span, stride=block), :] = moved[
-                    e * n_span : (e + 1) * n_span
-                ]
+        for first in range(0, depth, 8):
+            moved = []
+            for plane in range(first, first + 8):
+                high, low = split(source_ref[pl.ds(h * 128 * depth + plane, 128, stride=depth), :])
+                moved.append(dot(place, high, NT_DIMS) + dot(place, low, NT_DIMS))
+            turned_planes = jnp.transpose(jnp.stack(moved, axis=0), (1, 0, 2))
+            for slot in range(own):
+                e, p = divmod(slot, n_span)
+                sent_ref[pl.ds(p * block + (h * 4 + e) * depth + first, 8), :] = turned_planes[slot]
         send_phase(sent_ref, values_ref, out_send, out_recv, h)
 
     small_ref[...] = jnp.zeros_like(small_ref)
@@ -385,19 +423,32 @@
     out_trace = spread(traces_hot[0], traces_hot[1]) * trace_mask
     in_trace = spread(traces_hot[2], traces_hot[3]) * (COUPLING * trace_mask)
 
+    sides = []
+    for e in range(4):
+        a, b = divmod(e, 2)
+        groups = [0] * 4
+        groups[b], groups[1 - b] = (SOUTH, NORTH) if a == 0 else (NORTH, SOUTH)
+        groups[2 + a], groups[3 - a] = (WEST, EAST) if b == 0 else (EAST, WEST)
+        sides.append(groups)
+
     def turned(matrix, e):
-        turn = jnp.full((32, LANES), turn_ref[e * n_span + span], jnp.int32)
+        edge = ((turn_ref[e * n_span + span] >> shift) + 3) & 3
+        turn = jnp.full((32, LANES), edge, jnp.int32)
         edges = [matrix[d * 32 : (d + 1) * 32] for d in range(4)]
         blocks = []
-        for d in range(4):
+        for d in sides[e]:
             chosen = edges[d]
             for r in range(1, 4):
                 chosen = jnp.where(turn == r, edges[(d + r) % 4], chosen)
             blocks.append(chosen)
         return split(jnp.concatenate(blocks, axis=0))
 
-    to_trace = [turned(out_trace, e) for e in range(4)]
-    from_trace = [turned(in_trace, e) for e in range(4)]
+    to_trace, from_trace = [], []
+    for e in range(4):
+        high, low = turned(out_trace, e)
+        to_trace.append(jnp.concatenate([high, low], axis=0))
+        high, low = turned(in_trace, e)
+        from_trace.append((jnp.concatenate([high, high], axis=0), low))
 
     eig_row = small_ref[128:136, :]
     diag = (pick_right(eig_row, hot_i) + pick_right(eig_row, hot_j))[:1]
@@ -457,52 +508,50 @@
         g_rows = pl.ds(g * group, group)
         traces = []
         for e in range(4):
-            trace = dot3(split(modal_ref[e, g_rows, :]), to_trace[e], NT_DIMS)
+            high, low = split(modal_ref[e, g_rows, :])
+            both = dot(high, to_trace[e], NT_DIMS)
+            trace = both[:, :128] + both[:, 128:] + dot(low, to_trace[e][:128], NT_DIMS)
             trace_ref[e, g_rows, :] = trace
             traces.append(trace)
         for d in range(4):
-            packed = None
-            for h in range(2):
-                for q in range(2):
-                    piece = traces[outer[d][q]][h * half : (h + 1) * half]
-                    goal = h * 2 + q
-                    shift = (goal - d) % 4 * 32
-                    if shift:
-                        piece = pltpu.roll(piece, shift, 1)
-                    packed = piece if packed is None else jnp.where(lane_group == goal, piece, packed)
-            send_ref[sweep, g, d] = packed
+            one, two = (traces[i] for i in outer[d])
+            first, second = (0, 1) if d in (NORTH, SOUTH) else (2, 3)
+            joined = jnp.where(lane_group == first, one, two)
+            low_half = jnp.logical_or(lane_group == first, lane_group == second)
+            send_ref[sweep, g, d] = jnp.where(low_half, joined[:half], pltpu.roll(joined[half:], 64, 1))
         for copy in copies(sweep, g):
             copy.start()
 
     def update(sweep, g):
         for copy in copies(sweep, g):
             copy.wait_recv()
-        for h in range(2):
-            h_rows = pl.ds(g * group + h * half, half)
-            active = rounds_col[h_rows, :] > sweep + 1.5
-            active = jnp.concatenate([active, active], axis=1)
-            scale = inverse_ref[h_rows, :]
-            for e in range(4):
-                a, b = divmod(e, 2)
-                across = None
-                sides = (
-                    (NORTH, None) if a == 0 else (NORTH, b),
-                    (SOUTH, b) if a == 0 else (SOUTH, None),
-                    (EAST, None) if b == 0 else (EAST, a),
-                    (WEST, a) if b == 0 else (WEST, None),
-                )
-                for d, q in sides:
-                    if q is None:
-                        other = (2 * (1 - a) + b) if d in (NORTH, SOUTH) else (2 * a + 1 - b)
-                        piece = pltpu.roll(trace_ref[other, h_rows, :], 64, 1)
-                    else:
-                        piece = recv_ref[sweep, g, d]
-                        shift = (d - (h * 2 + q)) % 4 * 32
-                        if shift:
-                            piece = pltpu.roll(piece, shift, 1)
-                    across = piece if across is None else jnp.where(lane_group == d, piece, across)
-                fresh = (rhs_ref[e, h_rows, :] + dot3(split(across), from_trace[e])) * scale
-                modal_ref[e, h_rows, :] = jnp.where(active, fresh, modal_ref[e, h_rows, :])
+        g_rows = pl.ds(g * group, group)
+        active = rounds_col[g_rows, :] > sweep + 1.5
+        active = jnp.concatenate([active, active], axis=1)
+        scale = inverse_ref[g_rows, :]
+        outside = []
+        for d in range(4):
+            packed = recv_ref[sweep, g, d]
+            outside.append(jnp.concatenate([packed, pltpu.roll(packed, 64, 1)], axis=0))
+        for e in range(4):
+            a, b = divmod(e, 2)
+            across = jnp.where(
+                lane_group < 2,
+                jnp.where(
+                    lane_group == b,
+                    outside[SOUTH if a == 0 else NORTH],
+                    trace_ref[2 * (1 - a) + b, g_rows, :],
+                ),
+                jnp.where(
+                    lane_group == 2 + a,
+                    outside[WEST if b == 0 else EAST],
+                    trace_ref[2 * a + 1 - b, g_rows, :],
+                ),
+            )
+            high, low = split(across)
+            change = dot(jnp.concatenate([high, low], axis=1), from_trace[e][0]) + dot(high, from_trace[e][1])
+            fresh = (rhs_ref[e, g_rows, :] + change) * scale
+            modal_ref[e, g_rows, :] = jnp.where(active, fresh, modal_ref[e, g_rows, :])
 
     for g in range(GROUPS):
         g_rows = pl.ds(g * group, group)
@@ -541,18 +590,18 @@
                         back_ref[pl.ds(goal, depth), :] = value[
                             d * depth : (d + 1) * depth, i * 128 : (i + 1) * 128
                         ]
-        send_phase(back_ref, result_ref, back_send, back_recv, h)
-    for k in range(1, n_elem):
-        table_copy(k).wait_send()
+        send_phase(back_ref, (result_ref, second_ref), back_send, back_recv, h)
     for h in range(2):
         wait_phase(sent_ref, values_ref, out_send, out_recv, h, True)
     for sweep in range(SWEEPS):
         for g in range(GROUPS):
             for copy in copies(sweep, g):
                 copy.wait_send()
-    for h in range(2):
-        wait_phase(back_ref, result_ref, back_send, back_recv, h, True)
-        wait_phase(back_ref, result_ref, back_send, back_recv, h, False)
+    wait_phase(back_ref, (result_ref, second_ref), back_send, back_recv, 0, False)
+    place_back(n_span, depth, 0, result_ref, 4 * depth, place, half_ref)
+    wait_phase(back_ref, (result_ref, second_ref), back_send, back_recv, 0, True)
+    wait_phase(back_ref, (result_ref, second_ref), back_send, back_recv, 1, True)
+    wait_phase(back_ref, (result_ref, second_ref), back_send, back_recv, 1, False)
 
 
 def vmem():
@@ -578,20 +627,28 @@
     hot, mask = selection_tables()
     halo = (SWEEPS, GROUPS, 4, planes // GROUPS // 2, 128)
     dma = pltpu.SemaphoreType.DMA
-    returned, place = pl.pallas_call(
+    tables = pl.pallas_call(
+        functools.partial(table_kernel, n_elem, own),
+        out_shape=jax.ShapeDtypeStruct((n_elem * 8, own), jnp.int32),
+        in_specs=[vmem(), vmem()],
+        out_specs=vmem(),
+        scratch_shapes=[dma((n_elem,)), dma((n_elem,))],
+        compiler_params=pltpu.CompilerParams(collective_id=1, has_side_effects=True),
+        name="tables",
+    )(adjacency.T, edge_map.T).reshape(n_elem * 8 * own)
+    first_half, second_half, place = pl.pallas_call(
         functools.partial(main_kernel, n_span, n_elem, depth, own, MESH_X),
         out_shape=(
-            jax.ShapeDtypeStruct((flat, 128), F32),
+            jax.ShapeDtypeStruct((128 * depth, own), F32),
+            jax.ShapeDtypeStruct((flat // 2, 128), F32),
             jax.ShapeDtypeStruct((own, own), F32),
         ),
-        in_specs=[hbm(), hbm(), smem(), smem()] + [vmem()] * 7 + [hbm(), hbm()],
-        out_specs=(vmem(), vmem()),
+        in_specs=[hbm(), hbm(), smem(), smem()] + [vmem()] * 3 + [smem()] + [vmem()] * 2 + [hbm(), hbm()],
+        out_specs=(vmem(), vmem(), vmem()),
         scratch_shapes=[
             pltpu.VMEM((NS * depth, own), F32),
             pltpu.VMEM((NS * depth, own), F32),
             pltpu.VMEM((LANES * depth, own), F32),
-            pltpu.VMEM((n_elem * 8, own), jnp.int32),
-            pltpu.SMEM((n_elem * 8, own), jnp.int32),
             pltpu.SMEM((own,), jnp.int32),
             pltpu.VMEM((136, 128), F32),
             pltpu.VMEM((2, planes, planes), BF16),
@@ -599,6 +656,7 @@
             pltpu.VMEM((flat, 128), F32),
             pltpu.VMEM((flat, 128), F32),
             pltpu.VMEM((flat, 128), F32),
+            pltpu.VMEM((flat // 2, 128), F32),
             pltpu.VMEM((planes, 4 * LANES), BF16),
             pltpu.VMEM((planes, 4 * LANES), BF16),
             pltpu.VMEM((4, planes, LANES), F32),
@@ -609,9 +667,6 @@
             pltpu.VMEM(halo, F32),
             pltpu.VMEM(halo, F32),
             dma((6,)),
-            dma,
-            dma((n_elem,)),
-            dma((n_elem,)),
             dma((2, n_span)),
             dma((2, n_span)),
             dma((2, n_span)),
@@ -631,8 +686,7 @@
         stiff_eig.reshape(1, PER_SIDE),
         basis,
         rounds.reshape(1, planes // 2),
-        adjacency.T,
-        edge_map.T,
+        tables,
         hot,
         mask,
         split_table(forward),
@@ -641,11 +695,16 @@
     updated = pl.pallas_call(
         functools.partial(finish_kernel, n_span, depth, own),
         out_shape=jax.ShapeDtypeStruct((NS * depth, own), F32),
-        in_specs=[vmem(), vmem()],
-        out_specs=vmem(),
-        compiler_params=pltpu.CompilerParams(vmem_limit_bytes=VMEM_LIMIT),
+        in_specs=[hbm(), hbm(), vmem()],
+        out_specs=hbm(),
+        scratch_shapes=[
+            pltpu.VMEM((128 * depth, own), F32),
+            pltpu.VMEM((flat // 2, 128), F32),
+            pltpu.VMEM((NS * depth - 128 * depth, own), F32),
+            dma((4,)),
+        ],
         name="finish",
-    )(returned, place)
+    )(first_half, second_half, place)
     return updated.reshape(species.shape)
 
 

time: 145 us -> 144 us (level)
  Pallas kernels: 145 us -> 143 us
    pallas_call x1, Pallas kernels: 140 us -> 132 us  [body(): pl.pallas_call(functools.partial(main_kernel, n_span, n_elem, depth, own,...]
    pallas_call x0 -> x1, Pallas kernels: none -> 7.61 us  [body(): pl.pallas_call(functools.partial(table_kernel, n_elem, own), out_shape=ja...]
where the time goes in v3:
time: 144 us
  Pallas kernels  143 us (99%)
    pallas_call x1, Pallas kernels, body(): pl.pallas_call(functools.partial(main_kernel, n_span, n_elem, depth, own,...  132 us
    pallas_call x1, Pallas kernels, body(): pl.pallas_call(functools.partial(table_kernel, n_elem, own), out_shape=ja...  7.61 us
    pallas_call x1, Pallas kernels, body(): pl.pallas_call(functools.partial(finish_kernel, n_span, depth, own), out_...  4.04 us

profile of v3, /device:TPU:6, one launch (start us, length us, event | category | flops | bytes accessed | tf_op | source)
XLA Modules:
  0.0 143.5 jit_solution(4774816173157033401)
XLA Ops:
  0.0 7.6 %tables.1 = s32[64,128]{1,0:T(8,128)} custom-call(s32[4,128]{1,0:T(4,128)} %bitcast.11, s32[4,128]{1,0:T(4,128)} %bitcast.12), custom_call_target="tpu_custom_call" | custom-call | tf_op jit(solution)/shard_map/tables/pallas_call | solution.py:630
  7.6 131.7 %main.1 = (f32[2048,128]{1,0:T(8,128)}, f32[2048,128]{1,0:T(8,128)}, f32[128,128]{1,0:T(8,128)}) custom-call(f32[3888,128]{1,0:T(8,128)} %bitcast.8, f32[3888,128]{1,0:T(8,128)} %bitcast.9, f32[3,4]{1,0:T(4,128)} %binary_ref.1, f32[3]{0:T(128)} %dref_ref.1, f32[1,9]{1,0:T(1,128)} %bitcast.14, f32[9,9]{1,0:T(8,128)} %basis_ref.1, s32[1,256]{1,0:T(1,128)} %bitcast.13, ...), custom_call_target="tpu_custom_call" | custom-call | tf_op jit(solution)/shard_map/main/pallas_call | solution.py:639
  139.3 4.0 %finish.1 = f32[3888,128]{1,0:T(8,128)} custom-call(f32[2048,128]{1,0:T(8,128)} %get-tuple-element.8.half_hbm, f32[2048,128]{1,0:T(8,128)} %get-tuple-element.9.values_hbm, f32[128,128]{1,0:T(8,128)} %get-tuple-element.10.place_ref), custom_call_target="tpu_custom_call" | custom-call | tf_op jit(solution)/shard_map/finish/pallas_call | solution.py:695

commit v4 on v3

--- a/solution.py
+++ b/solution.py
@@ -53,29 +53,22 @@
 
 def selection_tables():
     pair = np.zeros((2, LANES, 128), np.float32)
-    pair_s = np.full((LANES,), -1)
     for lane in range(NS):
         node, s = divmod(lane, SPECIES)
         pair[0, lane, node // PER_SIDE] = 1.0
         pair[1, lane, node % PER_SIDE] = 1.0
-        pair_s[lane] = s
     trace = np.zeros((4, 128, 128), np.float32)
-    trace_s = np.full((128,), -2)
     for d, nodes in enumerate(edge_lists()):
         for t in range(PER_SIDE):
             for s in range(SPECIES):
                 lane = d * 32 + t * SPECIES + s
-                trace_s[lane] = s
                 back = nodes[PER_SIDE - 1 - t]
                 trace[0, lane, nodes[t] // PER_SIDE] = 1.0
                 trace[1, lane, nodes[t] % PER_SIDE] = 1.0
                 trace[2, lane, back // PER_SIDE] = 1.0
                 trace[3, lane, back % PER_SIDE] = 1.0
-    pair_mask = (pair_s[:, None] == pair_s[None, :]) & (pair_s[:, None] >= 0)
-    trace_mask = trace_s[:, None] == pair_s[None, :]
     hot = np.concatenate([pair.reshape(2 * LANES, 128), trace.reshape(512, 128)], axis=0)
-    mask = np.concatenate([pair_mask, trace_mask], axis=0)
-    return jnp.asarray(hot.astype(BF16)), jnp.asarray(mask.astype(np.float32))
+    return jnp.asarray(hot.astype(BF16))
 
 
 def transform_tables(planes):
@@ -83,9 +76,7 @@
     phase = (np.arange(modes)[:, None] * np.arange(planes)[None, :]) % planes
     angle = phase.astype(np.float64) * (2.0 * np.pi / planes)
     trig = np.concatenate([np.cos(angle), -np.sin(angle)], axis=0)
-    weight = np.where(np.arange(modes) == 0, 1.0, 2.0)
-    weight = np.concatenate([weight, weight])
-    return np.float32(trig / planes), np.float32((trig * weight[:, None]).T)
+    return np.float32(trig / planes)
 
 
 def split_table(table):
@@ -216,9 +207,7 @@
     rounds_ref,
     walk_ref,
     hot_ref,
-    mask_ref,
     forward_hbm,
-    backward_hbm,
     half_ref,
     second_ref,
     place_ref,
@@ -293,12 +282,8 @@
             copy = pltpu.make_async_copy(source.at[span_rows], target.at[span_rows], load_sem.at[i * 2 + j])
             copy.start()
             loads.append(copy)
-    table_loads = [
-        pltpu.make_async_copy(forward_hbm, forward_ref, load_sem.at[4]),
-        pltpu.make_async_copy(backward_hbm, backward_ref, load_sem.at[5]),
-    ]
-    for copy in table_loads:
-        copy.start()
+    table_load = pltpu.make_async_copy(forward_hbm, forward_ref, load_sem.at[4])
+    table_load.start()
 
     inverse = [[1.0 / binary_ref[s, j] for j in range(SPECIES + 1)] for s in range(SPECIES)]
     dref = [dref_ref[s] for s in range(SPECIES)]
@@ -418,10 +403,15 @@
         return pick_right(pick(left_i, basis), hot_i) * pick_right(pick(left_j, basis), hot_j)
 
     traces_hot = [hot_ref[pl.ds(2 * LANES + i * 128, 128), :] for i in range(4)]
-    trace_mask = mask_ref[LANES:, :]
-    pair = split(spread(hot_i, hot_j) * mask_ref[:LANES, :])
-    out_trace = spread(traces_hot[0], traces_hot[1]) * trace_mask
-    in_trace = spread(traces_hot[2], traces_hot[3]) * (COUPLING * trace_mask)
+
+    def same_species(shape, width):
+        left = lax.broadcasted_iota(jnp.int32, shape, 0) % width % SPECIES
+        return left == lax.broadcasted_iota(jnp.int32, shape, 1) % SPECIES
+
+    pair_same, trace_same = same_species((LANES, LANES), LANES), same_species((128, LANES), 32)
+    pair = split(jnp.where(pair_same, spread(hot_i, hot_j), 0.0))
+    out_trace = jnp.where(trace_same, spread(traces_hot[0], traces_hot[1]), 0.0)
+    in_trace = jnp.where(trace_same, COUPLING * spread(traces_hot[2], traces_hot[3]), 0.0)
 
     sides = []
     for e in range(4):
@@ -466,7 +456,12 @@
     rounds_col[:modes, :] = column
     rounds_col[modes:, :] = column
 
-    table_loads[0].wait()
+    table_load.wait()
+    for part in range(2):
+        for first in range(0, planes, min(128, planes)):
+            strip = pl.ds(first, min(128, planes))
+            turned_strip = forward_ref[part, strip, :].astype(F32).T
+            backward_ref[part, :, strip] = turned_strip.astype(BF16)
     for h in range(2):
         wait_phase(sent_ref, values_ref, out_send, out_recv, h, False)
         for e in (0, 2):
@@ -505,7 +500,7 @@
         ]
 
     def send_traces(sweep, g):
-        g_rows = pl.ds(g * group, group)
+        g_rows = pl.ds(pl.multiple_of(g * group, group), group)
         traces = []
         for e in range(4):
             high, low = split(modal_ref[e, g_rows, :])
@@ -525,8 +520,8 @@
     def update(sweep, g):
         for copy in copies(sweep, g):
             copy.wait_recv()
-        g_rows = pl.ds(g * group, group)
-        active = rounds_col[g_rows, :] > sweep + 1.5
+        g_rows = pl.ds(pl.multiple_of(g * group, group), group)
+        active = rounds_col[g_rows, :] > jnp.asarray(sweep, F32) + 1.5
         active = jnp.concatenate([active, active], axis=1)
         scale = inverse_ref[g_rows, :]
         outside = []
@@ -553,8 +548,8 @@
             fresh = (rhs_ref[e, g_rows, :] + change) * scale
             modal_ref[e, g_rows, :] = jnp.where(active, fresh, modal_ref[e, g_rows, :])
 
-    for g in range(GROUPS):
-        g_rows = pl.ds(g * group, group)
+    def begin(g, carry):
+        g_rows = pl.ds(pl.multiple_of(g * group, group), group)
         scale = inverse_ref[g_rows, :]
         for e in range(4):
             lanes = pl.ds(e * LANES, LANES)
@@ -562,19 +557,32 @@
             rhs_ref[e, g_rows, :] = rhs
             modal_ref[e, g_rows, :] = rhs * scale
         send_traces(0, g)
-    for sweep in range(SWEEPS):
-        for g in range(GROUPS):
-            update(sweep, g)
-            if sweep + 1 < SWEEPS:
-                send_traces(sweep + 1, g)
-
-    for e in range(4):
-        for first in range(0, planes, tile):
-            out_rows = pl.ds(first, tile)
-            high, low = split(dot3(split(modal_ref[e, out_rows, :]), pair, NT_DIMS))
+        return carry
+
+    def sweep_on(i, carry):
+        sweep, g = i // GROUPS, i % GROUPS
+        update(sweep, g)
+        send_traces(sweep + 1, g)
+        return carry
+
+    def sweep_last(g, carry):
+        update(SWEEPS - 1, g)
+        return carry
+
+    lax.fori_loop(0, GROUPS, begin, 0)
+    lax.fori_loop(0, (SWEEPS - 1) * GROUPS, sweep_on, 0)
+    lax.fori_loop(0, GROUPS, sweep_last, 0)
+
+    tile_row = lax.broadcasted_iota(jnp.int32, (tile, LANES), 0)
+    for first in range(0, planes, tile):
+        out_rows = pl.ds(first, tile)
+        column = tile_row + first
+        constant = jnp.logical_or(column == 0, column == modes)
+        weight = jnp.where(constant, float(planes), float(2 * planes))
+        for e in range(4):
+            high, low = split(dot3(split(modal_ref[e, out_rows, :]), pair, NT_DIMS) * weight)
             work_high[out_rows, pl.ds(e * LANES, LANES)] = high
             work_low[out_rows, pl.ds(e * LANES, LANES)] = low
-    table_loads[1].wait()
     for h in range(2):
         for e in (0, 2):
             lanes = [pl.ds((e + i) * LANES + h * 128, 128) for i in range(2)]
@@ -593,10 +601,13 @@
         send_phase(back_ref, (result_ref, second_ref), back_send, back_recv, h)
     for h in range(2):
         wait_phase(sent_ref, values_ref, out_send, out_recv, h, True)
-    for sweep in range(SWEEPS):
-        for g in range(GROUPS):
-            for copy in copies(sweep, g):
-                copy.wait_send()
+
+    def sent_traces(i, carry):
+        for copy in copies(i // GROUPS, i % GROUPS):
+            copy.wait_send()
+        return carry
+
+    lax.fori_loop(0, SWEEPS * GROUPS, sent_traces, 0)
     wait_phase(back_ref, (result_ref, second_ref), back_send, back_recv, 0, False)
     place_back(n_span, depth, 0, result_ref, 4 * depth, place, half_ref)
     wait_phase(back_ref, (result_ref, second_ref), back_send, back_recv, 0, True)
@@ -623,8 +634,8 @@
     own = species.shape[3]
     planes = depth * n_span
     flat = n_span * 8 * depth
-    forward, backward = transform_tables(planes)
-    hot, mask = selection_tables()
+    forward = transform_tables(planes)
+    hot = selection_tables()
     halo = (SWEEPS, GROUPS, 4, planes // GROUPS // 2, 128)
     dma = pltpu.SemaphoreType.DMA
     tables = pl.pallas_call(
@@ -643,7 +654,7 @@
             jax.ShapeDtypeStruct((flat // 2, 128), F32),
             jax.ShapeDtypeStruct((own, own), F32),
         ),
-        in_specs=[hbm(), hbm(), smem(), smem()] + [vmem()] * 3 + [smem()] + [vmem()] * 2 + [hbm(), hbm()],
+        in_specs=[hbm(), hbm(), smem(), smem()] + [vmem()] * 3 + [smem(), vmem(), hbm()],
         out_specs=(vmem(), vmem(), vmem()),
         scratch_shapes=[
             pltpu.VMEM((NS * depth, own), F32),
@@ -666,7 +677,7 @@
             pltpu.VMEM((4, planes, 128), F32),
             pltpu.VMEM(halo, F32),
             pltpu.VMEM(halo, F32),
-            dma((6,)),
+            dma((5,)),
             dma((2, n_span)),
             dma((2, n_span)),
             dma((2, n_span)),
@@ -688,9 +699,7 @@
         rounds.reshape(1, planes // 2),
         tables,
         hot,
-        mask,
         split_table(forward),
-        split_table(backward),
     )
     updated = pl.pallas_call(
         functools.partial(finish_kernel, n_span, depth, own),

time: 144 us -> 143 us (level)
  no operation moved by 1% of the time
where the time goes in v4:
time: 143 us; the launch traced here: 142 us
  Pallas kernels  142 us (99%)
    pallas_call x1, Pallas kernels, body(): pl.pallas_call(functools.partial(main_kernel, n_span, n_elem, depth, own,...  130 us
    pallas_call x1, Pallas kernels, body(): pl.pallas_call(functools.partial(table_kernel, n_elem, own), out_shape=ja...  7.61 us
    pallas_call x1, Pallas kernels, body(): pl.pallas_call(functools.partial(finish_kernel, n_span, depth, own), out_...  4.05 us

profile of v4, /device:TPU:6, one launch (start us, length us, event | category | flops | bytes accessed | tf_op | source)
XLA Modules:
  0.0 142.1 jit_solution(15301000482179722900)
XLA Ops:
  0.0 7.6 %tables.1 = s32[64,128]{1,0:T(8,128)} custom-call(s32[4,128]{1,0:T(4,128)} %bitcast.11, s32[4,128]{1,0:T(4,128)} %bitcast.12), custom_call_target="tpu_custom_call" | custom-call | tf_op jit(solution)/shard_map/tables/pallas_call | solution.py:641
  7.6 130.5 %main.1 = (f32[2048,128]{1,0:T(8,128)}, f32[2048,128]{1,0:T(8,128)}, f32[128,128]{1,0:T(8,128)}) custom-call(f32[3888,128]{1,0:T(8,128)} %bitcast.8, f32[3888,128]{1,0:T(8,128)} %bitcast.9, f32[3,4]{1,0:T(4,128)} %binary_ref.1, f32[3]{0:T(128)} %dref_ref.1, f32[1,9]{1,0:T(1,128)} %bitcast.14, f32[9,9]{1,0:T(8,128)} %basis_ref.1, s32[1,256]{1,0:T(1,128)} %bitcast.13, ...), custom_call_target="tpu_custom_call" | custom-call | tf_op jit(solution)/shard_map/main/pallas_call | solution.py:650
  138.1 4.0 %finish.1 = f32[3888,128]{1,0:T(8,128)} custom-call(f32[2048,128]{1,0:T(8,128)} %get-tuple-element.8.half_hbm, f32[2048,128]{1,0:T(8,128)} %get-tuple-element.9.values_hbm, f32[128,128]{1,0:T(8,128)} %get-tuple-element.10.place_ref), custom_call_target="tpu_custom_call" | custom-call | tf_op jit(solution)/shard_map/finish/pallas_call | solution.py:704

commit v5 on v4

--- a/solution.py
+++ b/solution.py
@@ -155,43 +155,6 @@
     }
 
 
-def table_kernel(n_elem, own, adjacency_ref, edge_map_ref, tables_ref, table_send, table_recv):
-    span, elem = lax.axis_index("span"), lax.axis_index("elem")
-    barrier = pltpu.get_barrier_semaphore()
-    for k in range(1, n_elem):
-        pl.semaphore_signal(
-            barrier, inc=1, device_id=(span, (elem + k) % n_elem), device_id_type=MESH
-        )
-
-    ahead_id, ahead_edge = adjacency_ref[...], edge_map_ref[...]
-    owner = ahead_id // own
-    step = owner * (8 * own) + (ahead_edge + 2) % 4 * own + ahead_id % own
-    before = (elem + n_elem - 1) % n_elem
-    edge_ids = lax.broadcasted_iota(jnp.int32, (4, own), 0)
-    elem_ids = lax.broadcasted_iota(jnp.int32, (4, own), 1)
-    facing = jnp.where(owner == before, (edge_ids + 2) % 4 * own + elem_ids, 8 * own)
-    start = jnp.min(jnp.min(facing, axis=0, keepdims=True), axis=1, keepdims=True)
-    my_rows = pl.ds(pl.multiple_of(elem * 8, 8), 8)
-    tables_ref[my_rows, :] = jnp.concatenate([step, jnp.broadcast_to(start, (4, own))], axis=0)
-
-    pl.semaphore_wait(barrier, n_elem - 1)
-
-    def table_copy(k):
-        return pltpu.make_async_remote_copy(
-            src_ref=tables_ref.at[my_rows],
-            dst_ref=tables_ref.at[my_rows],
-            send_sem=table_send.at[k],
-            recv_sem=table_recv.at[k],
-            device_id=(span, (elem + k) % n_elem),
-            device_id_type=MESH,
-        )
-
-    for k in range(1, n_elem):
-        table_copy(k).start()
-    for k in range(1, n_elem):
-        table_copy(k).wait()
-
-
 def main_kernel(
     n_span,
     n_elem,
@@ -205,7 +168,8 @@
     eig_ref,
     basis_ref,
     rounds_ref,
-    walk_ref,
+    adjacency_ref,
+    edge_map_ref,
     hot_ref,
     forward_hbm,
     half_ref,
@@ -214,6 +178,8 @@
     species_ref,
     laplacian_ref,
     source_ref,
+    tables_ref,
+    walk_ref,
     turn_ref,
     small_ref,
     forward_ref,
@@ -232,6 +198,9 @@
     send_ref,
     recv_ref,
     load_sem,
+    walk_sem,
+    table_send,
+    table_recv,
     out_send,
     out_recv,
     back_send,
@@ -312,17 +281,47 @@
     loads[1].wait()
     sources(*pieces[0])
 
+    ahead_id, ahead_edge = adjacency_ref[...], edge_map_ref[...]
+    owner = ahead_id // own
+    step = owner * (8 * own) + (ahead_edge + 2) % 4 * own + ahead_id % own
+    before = (elem + n_elem - 1) % n_elem
+    edge_ids = lax.broadcasted_iota(jnp.int32, (4, own), 0)
+    elem_ids = lax.broadcasted_iota(jnp.int32, (4, own), 1)
+    facing = jnp.where(owner == before, (edge_ids + 2) % 4 * own + elem_ids, 8 * own)
+    start = jnp.min(jnp.min(facing, axis=0, keepdims=True), axis=1, keepdims=True)
+    my_rows = pl.ds(pl.multiple_of(elem * 8, 8), 8)
+    tables_ref[my_rows, :] = jnp.concatenate([step, jnp.broadcast_to(start, (4, own))], axis=0)
+
+    pl.semaphore_wait(barrier, n_span + n_elem - 2)
+
+    def table_copy(k):
+        return pltpu.make_async_remote_copy(
+            src_ref=tables_ref.at[my_rows],
+            dst_ref=tables_ref.at[my_rows],
+            send_sem=table_send.at[k],
+            recv_sem=table_recv.at[k],
+            device_id=(span, (elem + k) % n_elem),
+            device_id_type=MESH,
+        )
+
+    for k in range(1, n_elem):
+        table_copy(k).start()
     loads[2].wait()
     loads[3].wait()
     sources(*pieces[1])
+    for k in range(1, n_elem):
+        table_copy(k).wait_recv()
+    walk = pltpu.make_async_copy(tables_ref, walk_ref, walk_sem)
+    walk.start()
+    walk.wait()
 
     shift = own.bit_length() - 1
 
     def ahead(dart):
-        return walk_ref[dart]
+        return walk_ref[dart >> shift, dart & (own - 1)]
 
     odd = elem % 2
-    dart = lax.fori_loop(0, rows * elem, lambda i, d: ahead(d), walk_ref[4 * own])
+    dart = lax.fori_loop(0, rows * elem, lambda i, d: ahead(d), walk_ref[4, 0])
     norths = []
     for row in range(rows):
         norths.append(dart)
@@ -379,7 +378,6 @@
 
         lax.fori_loop(1, n_span, one, 0)
 
-    pl.semaphore_wait(barrier, n_span + n_elem - 2)
     place = place_ref[...].astype(BF16)
     for h in range(2):
         for first in range(0, depth, 8):
@@ -573,17 +571,19 @@
     lax.fori_loop(0, (SWEEPS - 1) * GROUPS, sweep_on, 0)
     lax.fori_loop(0, GROUPS, sweep_last, 0)
 
-    tile_row = lax.broadcasted_iota(jnp.int32, (tile, LANES), 0)
-    for first in range(0, planes, tile):
-        out_rows = pl.ds(first, tile)
-        column = tile_row + first
-        constant = jnp.logical_or(column == 0, column == modes)
-        weight = jnp.where(constant, float(planes), float(2 * planes))
-        for e in range(4):
-            high, low = split(dot3(split(modal_ref[e, out_rows, :]), pair, NT_DIMS) * weight)
-            work_high[out_rows, pl.ds(e * LANES, LANES)] = high
-            work_low[out_rows, pl.ds(e * LANES, LANES)] = low
+    tile_row = lax.broadcasted_iota(jnp.int32, (tile, 128), 0)
     for h in range(2):
+        half_pair = tuple(part[h * 128 : (h + 1) * 128] for part in pair)
+        for first in range(0, planes, tile):
+            out_rows = pl.ds(first, tile)
+            column = tile_row + first
+            constant = jnp.logical_or(column == 0, column == modes)
+            weight = jnp.where(constant, float(planes), float(2 * planes))
+            for e in range(4):
+                lanes = pl.ds(e * LANES + h * 128, 128)
+                high, low = split(dot3(split(modal_ref[e, out_rows, :]), half_pair, NT_DIMS) * weight)
+                work_high[out_rows, lanes] = high
+                work_low[out_rows, lanes] = low
         for e in (0, 2):
             lanes = [pl.ds((e + i) * LANES + h * 128, 128) for i in range(2)]
             coeffs = tuple(
@@ -608,6 +608,8 @@
         return carry
 
     lax.fori_loop(0, SWEEPS * GROUPS, sent_traces, 0)
+    for k in range(1, n_elem):
+        table_copy(k).wait_send()
     wait_phase(back_ref, (result_ref, second_ref), back_send, back_recv, 0, False)
     place_back(n_span, depth, 0, result_ref, 4 * depth, place, half_ref)
     wait_phase(back_ref, (result_ref, second_ref), back_send, back_recv, 0, True)
@@ -638,15 +640,6 @@
     hot = selection_tables()
     halo = (SWEEPS, GROUPS, 4, planes // GROUPS // 2, 128)
     dma = pltpu.SemaphoreType.DMA
-    tables = pl.pallas_call(
-        functools.partial(table_kernel, n_elem, own),
-        out_shape=jax.ShapeDtypeStruct((n_elem * 8, own), jnp.int32),
-        in_specs=[vmem(), vmem()],
-        out_specs=vmem(),
-        scratch_shapes=[dma((n_elem,)), dma((n_elem,))],
-        compiler_params=pltpu.CompilerParams(collective_id=1, has_side_effects=True),
-        name="tables",
-    )(adjacency.T, edge_map.T).reshape(n_elem * 8 * own)
     first_half, second_half, place = pl.pallas_call(
         functools.partial(main_kernel, n_span, n_elem, depth, own, MESH_X),
         out_shape=(
@@ -654,12 +647,14 @@
             jax.ShapeDtypeStruct((flat // 2, 128), F32),
             jax.ShapeDtypeStruct((own, own), F32),
         ),
-        in_specs=[hbm(), hbm(), smem(), smem()] + [vmem()] * 3 + [smem(), vmem(), hbm()],
+        in_specs=[hbm(), hbm(), smem(), smem()] + [vmem()] * 6 + [hbm()],
         out_specs=(vmem(), vmem(), vmem()),
         scratch_shapes=[
             pltpu.VMEM((NS * depth, own), F32),
             pltpu.VMEM((NS * depth, own), F32),
             pltpu.VMEM((LANES * depth, own), F32),
+            pltpu.VMEM((n_elem * 8, own), jnp.int32),
+            pltpu.SMEM((n_elem * 8, own), jnp.int32),
             pltpu.SMEM((own,), jnp.int32),
             pltpu.VMEM((136, 128), F32),
             pltpu.VMEM((2, planes, planes), BF16),
@@ -678,6 +673,9 @@
             pltpu.VMEM(halo, F32),
             pltpu.VMEM(halo, F32),
             dma((5,)),
+            dma,
+            dma((n_elem,)),
+            dma((n_elem,)),
             dma((2, n_span)),
             dma((2, n_span)),
             dma((2, n_span)),
@@ -697,7 +695,8 @@
         stiff_eig.reshape(1, PER_SIDE),
         basis,
         rounds.reshape(1, planes // 2),
-        tables,
+        adjacency.T,
+        edge_map.T,
         hot,
         split_table(forward),
     )

time: 143 us -> 141 us (0.986)
    pallas_call x1 -> x0, Pallas kernels: 7.61 us -> none  [body(): pl.pallas_call(functools.partial(table_kernel, n_elem, own), out_shape=ja...]
    pallas_call x1, Pallas kernels: 130 us -> 137 us  [body(): pl.pallas_call(functools.partial(main_kernel, n_span, n_elem, depth, own,...]
where the time goes in v5:
time: 141 us
  Pallas kernels  141 us (100%)
    pallas_call x1, Pallas kernels, body(): pl.pallas_call(functools.partial(main_kernel, n_span, n_elem, depth, own,...  137 us
    pallas_call x1, Pallas kernels, body(): pl.pallas_call(functools.partial(finish_kernel, n_span, depth, own), out_...  4.05 us

profile of v5, /device:TPU:6, one launch (start us, length us, event | category | flops | bytes accessed | tf_op | source)
XLA Modules:
  0.0 140.9 jit_solution(18048506874403181059)
XLA Ops:
  0.0 136.8 %main.1 = (f32[2048,128]{1,0:T(8,128)}, f32[2048,128]{1,0:T(8,128)}, f32[128,128]{1,0:T(8,128)}) custom-call(f32[3888,128]{1,0:T(8,128)} %bitcast.7, f32[3888,128]{1,0:T(8,128)} %bitcast.8, f32[3,4]{1,0:T(4,128)} %binary_ref.1, f32[3]{0:T(128)} %dref_ref.1, f32[1,9]{1,0:T(1,128)} %bitcast.12, f32[9,9]{1,0:T(8,128)} %basis_ref.1, s32[1,256]{1,0:T(1,128)} %bitcast.11, ...), custom_call_target="tpu_custom_call" | custom-call | tf_op jit(solution)/shard_map/main/pallas_call | solution.py:643
  136.9 4.0 %finish.1 = f32[3888,128]{1,0:T(8,128)} custom-call(f32[2048,128]{1,0:T(8,128)} %get-tuple-element.8.half_hbm, f32[2048,128]{1,0:T(8,128)} %get-tuple-element.9.values_hbm, f32[128,128]{1,0:T(8,128)} %get-tuple-element.10.place_ref), custom_call_target="tpu_custom_call" | custom-call | tf_op jit(solution)/shard_map/finish/pallas_call | solution.py:703

commit v6 on v5

--- a/solution.py
+++ b/solution.py
@@ -116,30 +116,6 @@
             out_ref[pl.ds(lane * depth + first, 8), :] = by_lane[lane]
 
 
-def finish_kernel(
-    n_span, depth, own, half_hbm, values_hbm, place_ref, out_hbm, half_ref, values_ref, tail_ref, sems
-):
-    loads = [
-        pltpu.make_async_copy(values_hbm, values_ref, sems.at[0]),
-        pltpu.make_async_copy(half_hbm, half_ref, sems.at[1]),
-    ]
-    for copy in loads:
-        copy.start()
-    split_row = 128 * depth
-    stores = [
-        pltpu.make_async_copy(half_ref, out_hbm.at[pl.ds(0, split_row)], sems.at[2]),
-        pltpu.make_async_copy(tail_ref, out_hbm.at[pl.ds(split_row, NS * depth - split_row)], sems.at[3]),
-    ]
-    loads[1].wait()
-    stores[0].start()
-    place = place_ref[...].astype(BF16)
-    loads[0].wait()
-    place_back(n_span, depth, 1, values_ref, 4 * depth, place, tail_ref)
-    stores[1].start()
-    stores[0].wait()
-    stores[1].wait()
-
-
 def neighbours(n_span, n_elem, block_rows):
     span, elem = lax.axis_index("span"), lax.axis_index("elem")
     x = span % block_rows
@@ -172,7 +148,9 @@
     edge_map_ref,
     hot_ref,
     forward_hbm,
+    out_hbm,
     half_ref,
+    tail_ref,
     second_ref,
     place_ref,
     species_ref,
@@ -198,6 +176,7 @@
     send_ref,
     recv_ref,
     load_sem,
+    store_sem,
     walk_sem,
     table_send,
     table_recv,
@@ -611,10 +590,20 @@
     for k in range(1, n_elem):
         table_copy(k).wait_send()
     wait_phase(back_ref, (result_ref, second_ref), back_send, back_recv, 0, False)
+    split_row = 128 * depth
+    stores = [
+        pltpu.make_async_copy(half_ref, out_hbm.at[pl.ds(0, split_row)], store_sem.at[0]),
+        pltpu.make_async_copy(tail_ref, out_hbm.at[pl.ds(split_row, NS * depth - split_row)], store_sem.at[1]),
+    ]
     place_back(n_span, depth, 0, result_ref, 4 * depth, place, half_ref)
+    stores[0].start()
     wait_phase(back_ref, (result_ref, second_ref), back_send, back_recv, 0, True)
     wait_phase(back_ref, (result_ref, second_ref), back_send, back_recv, 1, True)
     wait_phase(back_ref, (result_ref, second_ref), back_send, back_recv, 1, False)
+    place_back(n_span, depth, 1, second_ref, 4 * depth, place, tail_ref)
+    stores[1].start()
+    stores[0].wait()
+    stores[1].wait()
 
 
 def vmem():
@@ -640,16 +629,16 @@
     hot = selection_tables()
     halo = (SWEEPS, GROUPS, 4, planes // GROUPS // 2, 128)
     dma = pltpu.SemaphoreType.DMA
-    first_half, second_half, place = pl.pallas_call(
+    updated = pl.pallas_call(
         functools.partial(main_kernel, n_span, n_elem, depth, own, MESH_X),
-        out_shape=(
-            jax.ShapeDtypeStruct((128 * depth, own), F32),
-            jax.ShapeDtypeStruct((flat // 2, 128), F32),
-            jax.ShapeDtypeStruct((own, own), F32),
-        ),
+        out_shape=jax.ShapeDtypeStruct((NS * depth, own), F32),
         in_specs=[hbm(), hbm(), smem(), smem()] + [vmem()] * 6 + [hbm()],
-        out_specs=(vmem(), vmem(), vmem()),
+        out_specs=hbm(),
         scratch_shapes=[
+            pltpu.VMEM((128 * depth, own), F32),
+            pltpu.VMEM((NS * depth - 128 * depth, own), F32),
+            pltpu.VMEM((flat // 2, 128), F32),
+            pltpu.VMEM((own, own), F32),
             pltpu.VMEM((NS * depth, own), F32),
             pltpu.VMEM((NS * depth, own), F32),
             pltpu.VMEM((LANES * depth, own), F32),
@@ -673,6 +662,7 @@
             pltpu.VMEM(halo, F32),
             pltpu.VMEM(halo, F32),
             dma((5,)),
+            dma((2,)),
             dma,
             dma((n_elem,)),
             dma((n_elem,)),
@@ -700,19 +690,6 @@
         hot,
         split_table(forward),
     )
-    updated = pl.pallas_call(
-        functools.partial(finish_kernel, n_span, depth, own),
-        out_shape=jax.ShapeDtypeStruct((NS * depth, own), F32),
-        in_specs=[hbm(), hbm(), vmem()],
-        out_specs=hbm(),
-        scratch_shapes=[
-            pltpu.VMEM((128 * depth, own), F32),
-            pltpu.VMEM((flat // 2, 128), F32),
-            pltpu.VMEM((NS * depth - 128 * depth, own), F32),
-            dma((4,)),
-        ],
-        name="finish",
-    )(first_half, second_half, place)
     return updated.reshape(species.shape)
 
 

time: 141 us -> 140 us (level)
  Pallas kernels: 141 us -> 137 us
  local copies, waits for them, and re-layouts: 0 us -> 2.97 us
    pallas_call x1 -> x0, Pallas kernels: 4.05 us -> none  [body(): pl.pallas_call(functools.partial(finish_kernel, n_span, depth, own), out_...]
    unnamed x0 -> x1, local copies, waits for them, and re-layouts: none -> 2.97 us
where the time goes in v6:
time: 140 us
  Pallas kernels  137 us (98%)
  local copies, waits for them, and re-layouts  2.97 us (2%)
    pallas_call x1, Pallas kernels, body(): pl.pallas_call(functools.partial(main_kernel, n_span, n_elem, depth, own,...  137 us
    unnamed x1, local copies, waits for them, and re-layouts  2.97 us

profile of v6, /device:TPU:6, one launch (start us, length us, event | category | flops | bytes accessed | tf_op | source)
XLA Modules:
  0.0 140.2 jit_solution(11057482223443048884)
XLA Ops:
  0.0 137.2 %main.1 = f32[3888,128]{1,0:T(8,128)} custom-call(f32[3888,128]{1,0:T(8,128)} %bitcast.8, f32[3888,128]{1,0:T(8,128)} %bitcast.9, f32[3,4]{1,0:T(4,128)} %binary_ref.1, f32[3]{0:T(128)} %dref_ref.1, f32[1,9]{1,0:T(1,128)} %bitcast.13, f32[9,9]{1,0:T(8,128)} %basis_ref.1, s32[1,256]{1,0:T(1,128)} %bitcast.12, s32[4,128]{1,0:T(4,128)} %bitcast.10, ...), custom_call_target="tpu_custom_call" | custom-call | tf_op jit(solution)/shard_map/main/pallas_call | solution.py:632
  137.2 3.0 %copy.13 = f32[81,3,16,128]{3,2,1,0:T(8,128)} copy(f32[81,3,16,128]{3,2,1,0:T(8,128)} %bitcast.7) | data formatting | bytes 3981312

commit v7 on v6

--- a/solution.py
+++ b/solution.py
@@ -525,14 +525,17 @@
             fresh = (rhs_ref[e, g_rows, :] + change) * scale
             modal_ref[e, g_rows, :] = jnp.where(active, fresh, modal_ref[e, g_rows, :])
 
-    def begin(g, carry):
-        g_rows = pl.ds(pl.multiple_of(g * group, group), group)
-        scale = inverse_ref[g_rows, :]
+    def into_basis(step, carry):
+        t_rows = pl.ds(pl.multiple_of(step * tile, tile), tile)
+        scale = inverse_ref[t_rows, :]
         for e in range(4):
             lanes = pl.ds(e * LANES, LANES)
-            rhs = dot3((work_high[g_rows, lanes], work_low[g_rows, lanes]), pair)
-            rhs_ref[e, g_rows, :] = rhs
-            modal_ref[e, g_rows, :] = rhs * scale
+            rhs = dot3((work_high[t_rows, lanes], work_low[t_rows, lanes]), pair)
+            rhs_ref[e, t_rows, :] = rhs
+            modal_ref[e, t_rows, :] = rhs * scale
+        return carry
+
+    def begin(g, carry):
         send_traces(0, g)
         return carry
 
@@ -546,6 +549,7 @@
         update(SWEEPS - 1, g)
         return carry
 
+    lax.fori_loop(0, planes // tile, into_basis, 0)
     lax.fori_loop(0, GROUPS, begin, 0)
     lax.fori_loop(0, (SWEEPS - 1) * GROUPS, sweep_on, 0)
     lax.fori_loop(0, GROUPS, sweep_last, 0)

time: 140 us -> 141 us (level)
  no operation moved by 1% of the time
where the time goes in v7:
time: 141 us
  Pallas kernels  138 us (98%)
  local copies, waits for them, and re-layouts  2.97 us (2%)
    pallas_call x1, Pallas kernels, body(): pl.pallas_call(functools.partial(main_kernel, n_span, n_elem, depth, own,...  138 us
    unnamed x1, local copies, waits for them, and re-layouts  2.97 us

profile of v7, /device:TPU:6, one launch (start us, length us, event | category | flops | bytes accessed | tf_op | source)
XLA Modules:
  0.0 141.2 jit_solution(4894321663594340212)
XLA Ops:
  0.0 138.2 %main.1 = f32[3888,128]{1,0:T(8,128)} custom-call(f32[3888,128]{1,0:T(8,128)} %bitcast.8, f32[3888,128]{1,0:T(8,128)} %bitcast.9, f32[3,4]{1,0:T(4,128)} %binary_ref.1, f32[3]{0:T(128)} %dref_ref.1, f32[1,9]{1,0:T(1,128)} %bitcast.13, f32[9,9]{1,0:T(8,128)} %basis_ref.1, s32[1,256]{1,0:T(1,128)} %bitcast.12, s32[4,128]{1,0:T(4,128)} %bitcast.10, ...), custom_call_target="tpu_custom_call" | custom-call | tf_op jit(solution)/shard_map/main/pallas_call | solution.py:636
  138.2 3.0 %copy.13 = f32[81,3,16,128]{3,2,1,0:T(8,128)} copy(f32[81,3,16,128]{3,2,1,0:T(8,128)} %bitcast.7) | data formatting | bytes 3981312
